TPU v7x, 32 devices: a whole 2x2x4 slice. The times are simulated.
32 devices in a mesh: dp: 16 (over z, y, x), tensor: 2 (over core).
Axes of the slice: x: 2, y: 2, z: 4, core: 2. Of those that a mesh axis runs over, the one named last changes fastest.
Arguments:
- tokens: bfloat16 [8192, 768], P('dp'), may hold values from -6 to 6
- segments: int32 [8192], P('dp'), may hold values from 0 to 8191, as said below
- routes: int32 [8192, 2], P('dp'), may hold values from 0 to 7, as said below
- prev_logits: float32 [8192, 8], P('dp'), may hold values from -3 to 3
- attn_gain: float32 [768], replicated, may hold values from 0.5 to 1.5
- w_qkv: bfloat16 [3, 768, 768], P(None, None, 'tensor'), may hold values from -0.21875 to 0.21875
- w_out: bfloat16 [768, 768], P('tensor'), may hold values from -1.75 to 1.75
- ffn_gain: float32 [768], replicated, may hold values from 0.5 to 1.5
- w_router: bfloat16 [768, 8], replicated, may hold values from -0.109375 to 0.109375
- w_const: bfloat16 [768, 4], replicated, may hold values from -0.21875 to 0.21875
- v_const: float32 [2, 768], replicated, may hold values from -6 to 6
- w_gu: bfloat16 [4, 2, 768, 2048], P(None, None, None, 'tensor'), may hold values from -0.21875 to 0.21875
- w_down: bfloat16 [4, 2048, 768], P(None, 'tensor'), may hold values from -0.75 to 0.75
- cotangent: bfloat16 [8192, 768], P('dp'), may hold values from -6 to 6
Outputs:
- output: bfloat16 [8192, 768], P('dp')
- tokens_grad: float32 [8192, 768], P('dp')
- prev_grad: float32 [8192, 8], P('dp')
- attn_gain_grad: float32 [768], P('dp')
- w_qkv_grad: float32 [3, 768, 768], P(None, 'dp', 'tensor')
- w_out_grad: float32 [768, 768], P('tensor', 'dp')
- ffn_gain_grad: float32 [768], P('dp')
- w_router_grad: float32 [768, 8], P('dp')
- w_const_grad: float32 [768, 4], P('dp')
- v_const_grad: float32 [2, 768], P(None, 'dp')
- w_gu_grad: float32 [4, 2, 768, 2048], P(None, None, 'dp', 'tensor')
- w_down_grad: float32 [4, 2048, 768], P(None, 'tensor', 'dp')
Inputs may be any that keep to these rules, and one draw needn't show every extreme that they name: `segments`: ids are non-decreasing along the tokens, and tokens of different packed sequences of 8192 tokens have different ids. `routes`: a token's two experts differ, and the first is a feed-forward expert, a number below 4.
All inputs are finite; a program needn't handle non-finite values.
Results may differ from a plain program's by a relative error of at most 0.019.
Values may be sent and summed in bfloat16 or wider, within the bound.
No kernel may reach another device: no remote copies, remote signals or barrier semaphores. Data moves between devices by JAX's collectives and lax.ppermute only.
A program may use at most 448 MiB of HBM per device.

v0:
```python
import functools
import math

import jax
import jax.numpy as jnp
import numpy as np
from jax import lax
from jax.experimental import pallas as pl
from jax.experimental.pallas import tpu as pltpu
from jax.sharding import Mesh
from jax.sharding import PartitionSpec as P

f32 = jnp.float32
bf = jnp.bfloat16
E_FFN = 4
NCONST = 2
E_ALL = 8
SPAN = 16
SEQ_LEN = 8192
EPSILON = 1e-05
HIGHEST = lax.Precision.HIGHEST
GROUP = ("z", "y", "x")
GATE_ROWS = 16


HD = 64
NEG = -1e30
WIDE = (4, 2, 1)


def dotf(a, b, ca, cb):
    return lax.dot_general(a, b, (((ca,), (cb,)), ((), ())), preferred_element_type=f32)


def key_places(t, blocks, half):
    r = lax.broadcasted_iota(jnp.int32, (blocks * 2 * half, half), 0)
    inside = r % (2 * half)
    return r - inside + jnp.where(inside < half, t * half + inside, (1 - t) * half + inside - half)


def fwd_kernel(nb, half, sc, start_ref, own_ref, oth_ref, o_ref, of_ref, lse_ref, ktm, vt):
    keys = 2 * half
    t = sc[0]

    def prep(j, _):
        at = pl.ds(pl.multiple_of(j * keys, keys), half)
        more = pl.ds(pl.multiple_of(j * keys + half, half), half)
        ktm[at, :] = own_ref[j, HD : 2 * HD, :].T
        ktm[more, :] = oth_ref[j, 0:HD, :].T
        vt[:, at] = own_ref[j, 2 * HD : 3 * HD, :]
        vt[:, more] = oth_ref[j, HD : 2 * HD, :]
        return 0

    lax.fori_loop(0, nb, prep, 0)
    lane = lax.broadcasted_iota(jnp.int32, (1, half), 1)

    def qblock(s, _):
        q = own_ref[s, 0:HD, :] * bf(0.125)
        start_row = start_ref[s]
        last_row = s * keys + t * half + lane
        lo, ml = sc[1 + s], jnp.minimum(sc[1 + nb + s], s)

        def scores(j, n):
            return dotf(ktm[pl.ds(pl.multiple_of(j * keys, keys), n * keys), :], q, 1, 0)

        def allowed(j, n):
            place = key_places(t, n, half) + j * keys
            return (place >= start_row) & (place <= last_row)

        def values(j, n):
            return vt[:, pl.ds(pl.multiple_of(j * keys, keys), n * keys)]

        def emit(o, lse):
            o_ref[s] = o.astype(bf)
            of_ref[s] = o
            lse_ref[s] = lse

        def plain(j, n, c, masked):
            l, acc = c
            p = jnp.exp(scores(j, n))
            if masked:
                p = jnp.where(allowed(j, n), p, 0.0)
            return l + jnp.sum(p, axis=0, keepdims=True), acc + dotf(values(j, n), p.astype(bf), 1, 0)

        c = (jnp.zeros((1, half), f32), jnp.zeros((HD, half), f32))
        c = plain(s, 1, c, True)
        for masked, first, end in ((True, lo, ml), (False, jnp.maximum(lo, ml), s)):
            for n in WIDE:
                count = jnp.maximum(end - first, 0) // n
                c = lax.fori_loop(0, count, lambda i, c: plain(first + i * n, n, c, masked), c)
                first = first + count * n
        l, acc = c
        emit(acc / l, jnp.log(l))
        fine = (jnp.min(l) > 1e-25) & (jnp.max(l) < 1e25)

        @pl.when(jnp.logical_not(fine))
        def _():
            def shifted(j, c):
                m, l, acc = c
                sco = jnp.where(allowed(j, 1), scores(j, 1), NEG)
                mn = jnp.maximum(m, jnp.max(sco, axis=0, keepdims=True))
                p = jnp.exp(sco - mn)
                al = jnp.exp(m - mn)
                return mn, l * al + jnp.sum(p, axis=0, keepdims=True), acc * al + dotf(values(j, 1), p.astype(bf), 1, 0)

            c = (jnp.full((1, half), NEG, f32), jnp.zeros((1, half), f32), jnp.zeros((HD, half), f32))
            c = shifted(s, c)
            m, l, acc = lax.fori_loop(lo, s, shifted, c)
            emit(acc / l, m + jnp.log(l))

        return 0

    lax.fori_loop(0, nb, qblock, 0)


def flash_fwd(sc, start, own, oth):
    nb, _, half = own.shape
    v = pl.BlockSpec(memory_space=pltpu.VMEM)
    return pl.pallas_call(
        functools.partial(fwd_kernel, nb, half),
        out_shape=(
            jax.ShapeDtypeStruct((nb, HD, half), bf),
            jax.ShapeDtypeStruct((nb, HD, half), f32),
            jax.ShapeDtypeStruct((nb, 1, half), f32),
        ),
        in_specs=[pl.BlockSpec(memory_space=pltpu.SMEM), v, v, v],
        out_specs=(v, v, v),
        scratch_shapes=[pltpu.VMEM((nb * 2 * half, HD), bf), pltpu.VMEM((HD, nb * 2 * half), bf)],
        compiler_params=pltpu.CompilerParams(vmem_limit_bytes=48 << 20),
        cost_estimate=pl.CostEstimate(flops=10**9, bytes_accessed=4 << 20, transcendentals=10**6),
        name="flash_fwd",
    )(sc, start, own, oth)


def bwd_kernel(
    nb, half, j0, j1, sc, start_ref, own_ref, oth_ref, do_ref, of_ref, lse_ref,
    dq_ref, dko_ref, dkx_ref, ktm, vtm, kt, qt, dot, dq_acc, dotm, qtm, stats,
):
    keys = 2 * half
    t = sc[0]

    def prep(j, _):
        k = j - j0
        ktm[k, 0:half, :] = own_ref[j, HD : 2 * HD, :].T
        ktm[k, half:keys, :] = oth_ref[j, 0:HD, :].T
        vtm[k, 0:half, :] = own_ref[j, 2 * HD : 3 * HD, :].T
        vtm[k, half:keys, :] = oth_ref[j, HD : 2 * HD, :].T
        kt[k, :, 0:half] = own_ref[j, HD : 2 * HD, :]
        kt[k, :, half:keys] = oth_ref[j, 0:HD, :]
        return 0

    lax.fori_loop(j0, j1, prep, 0)

    def prep_q(s, _):
        at = pl.ds(pl.multiple_of(s * half, half), half)
        q = own_ref[s, 0:HD, :] * bf(0.125)
        qt[:, at] = q
        qtm[at, :] = q.T
        dot[:, at] = do_ref[s]
        dotm[at, :] = do_ref[s].T
        dq_acc[:, at] = jnp.zeros((HD, half), f32)
        stats[0:1, at] = lse_ref[s]
        stats[1:2, at] = jnp.sum(do_ref[s].astype(f32) * of_ref[s], axis=0, keepdims=True)
        return 0

    lax.fori_loop(j0, nb, prep_q, 0)
    lane = lax.broadcasted_iota(jnp.int32, (1, half), 1)

    def kblock(j, _):
        k = j - j0
        kj, vj, ktj = ktm[k], vtm[k], kt[k]

        def tile(s, n, c, masked):
            dk, dv = c
            at = pl.ds(pl.multiple_of(s * half, half), n * half)
            sco = dotf(kj, qt[:, at], 1, 0)
            if masked:
                place = key_places(t, 1, half) + j * keys
                last_row = s * keys + t * half + lane
                sco = jnp.where((place >= start_ref[s]) & (place <= last_row), sco, NEG)
            p = jnp.exp(sco - stats[0:1, at])
            dp = dotf(vj, dot[:, at], 1, 0)
            ds = (p * (dp - stats[1:2, at])).astype(bf)
            dv = dv + dotf(p.astype(bf), dotm[at, :], 1, 0)
            dk = dk + dotf(ds, qtm[at, :], 1, 0)
            dq_acc[:, at] += dotf(ktj, ds, 1, 0)
            return dk, dv

        c = (jnp.zeros((keys, HD), f32), jnp.zeros((keys, HD), f32))
        c = tile(j, 1, c, True)
        mid, hi = sc[1 + 2 * nb + j], sc[1 + 3 * nb + j]
        first = j + 1
        for n in WIDE:
            count = jnp.maximum(mid - first, 0) // n
            c = lax.fori_loop(0, count, lambda i, c: tile(first + i * n, n, c, False), c)
            first = first + count * n
        dk, dv = lax.fori_loop(jnp.maximum(j + 1, mid), hi, lambda s, c: tile(s, 1, c, True), c)
        dk = dk.T
        dv = dv.T
        dko_ref[k, 0:HD, :] = dk[:, 0:half]
        dko_ref[k, HD : 2 * HD, :] = dv[:, 0:half]
        dkx_ref[k, 0:HD, :] = dk[:, half:keys].astype(bf)
        dkx_ref[k, HD : 2 * HD, :] = dv[:, half:keys].astype(bf)
        return 0

    lax.fori_loop(j0, j1, kblock, 0)

    def finish(s, _):
        at = pl.ds(pl.multiple_of(s * half, half), half)
        dq_ref[s] = (dq_acc[:, at] * 0.125).astype(bf)
        return 0

    def nothing(s, _):
        dq_ref[s] = jnp.zeros((HD, half), bf)
        return 0

    lax.fori_loop(0, j0, nothing, 0)
    lax.fori_loop(j0, nb, finish, 0)


def flash_bwd(sc, start, own, oth, do, of, lse, j0=0, j1=SPAN):
    nb, _, half = own.shape
    v = pl.BlockSpec(memory_space=pltpu.VMEM)
    n = j1 - j0
    return pl.pallas_call(
        functools.partial(bwd_kernel, nb, half, j0, j1),
        out_shape=(
            jax.ShapeDtypeStruct((nb, HD, half), bf),
            jax.ShapeDtypeStruct((n, 2 * HD, half), f32),
            jax.ShapeDtypeStruct((n, 2 * HD, half), bf),
        ),
        in_specs=[pl.BlockSpec(memory_space=pltpu.SMEM)] + [v] * 6,
        out_specs=(v, v, v),
        scratch_shapes=[
            pltpu.VMEM((n, 2 * half, HD), bf),
            pltpu.VMEM((n, 2 * half, HD), bf),
            pltpu.VMEM((n, HD, 2 * half), bf),
            pltpu.VMEM((HD, nb * half), bf),
            pltpu.VMEM((HD, nb * half), bf),
            pltpu.VMEM((HD, nb * half), f32),
            pltpu.VMEM((nb * half, HD), bf),
            pltpu.VMEM((nb * half, HD), bf),
            pltpu.VMEM((8, nb * half), f32),
        ],
        compiler_params=pltpu.CompilerParams(vmem_limit_bytes=56 << 20),
        cost_estimate=pl.CostEstimate(flops=10**9, bytes_accessed=4 << 20, transcendentals=10**6),
        name="flash_bwd",
    )(sc, start, own, oth, do, of, lse)


def bounds(start_all, t, nb, HB):
    st=start_all.reshape(nb,2,HB)
    mine=lax.dynamic_index_in_dim(st,t,1,keepdims=False)
    first=mine[:,0]; last=mine[:,HB-1]
    B=2*HB
    lo=first//B
    ml=(last+B-1)//B
    j=jnp.arange(nb)
    mid=jnp.sum((last[None,:]<=j[:,None]*B).astype(jnp.int32),axis=1)
    hi=jnp.sum((lo[None,:]<=j[:,None]).astype(jnp.int32),axis=1)
    mid=jnp.minimum(mid,hi)
    sc=jnp.concatenate([jnp.full((1,),t,jnp.int32),lo,ml,mid,hi]).astype(jnp.int32)
    return sc,mine[:,None,:]


def ffn_kernel(e_ref, u_ref, wgu_ref, wd_ref, *refs):
    pieces = refs[:8]
    x_out_ref, g_ref, wh_ref, mine_ref, other_ref, out_mine_ref, out_other_ref, held = refs[8:]
    half = u_ref.shape[1]
    width = x_out_ref.shape[2]
    hidden_units = wgu_ref.shape[3]
    e = e_ref[0]
    step = pl.program_id(0)
    for k in range(8):

        @pl.when(step == k)
        def _(k=k):
            held[...] = pieces[k][...]

    gates = held[half : half + GATE_ROWS, 0:half].astype(f32)
    row = lax.broadcasted_iota(jnp.int32, gates.shape, 0)
    gate_row = jnp.sum(jnp.where((row == e) | (row == e + E_FFN), gates, 0.0), axis=0, keepdims=True)
    gate = jnp.broadcast_to(gate_row, (8, half)).T[:, 0:1]
    x = held[0:half, :]
    x_out_ref[0] = x
    g = dotf(x, wgu_ref[0, 0], 1, 0)
    up = dotf(x, wgu_ref[0, 1], 1, 0)
    raw = u_ref[0].astype(f32)
    sig = 0.5 * jnp.tanh(0.5 * g) + 0.5
    silu = g * sig
    hid = silu * up
    hg = gate * raw
    g_ref[0, :, 0:hidden_units] = (hg * up * (sig + silu * (1.0 - sig))).astype(bf)
    g_ref[0, :, hidden_units : 2 * hidden_units] = (hg * silu).astype(bf)
    wh_ref[0] = (gate * hid).astype(bf)
    dots = jnp.broadcast_to(jnp.sum(hid * raw, axis=-1, keepdims=True), (half, 128)).T[0:8]
    total = dotf(g_ref[0, :, 0:hidden_units], wgu_ref[0, 0], 1, 1)
    total = total + dotf(g_ref[0, :, hidden_units : 2 * hidden_units], wgu_ref[0, 1], 1, 1)
    result = dotf(wh_ref[0], wd_ref[0], 1, 0)
    drow = lax.broadcasted_iota(jnp.int32, (GATE_ROWS, half), 0)
    placed = jnp.where(drow == e, jnp.broadcast_to(dots[0:1, :], (GATE_ROWS, half)), 0.0).astype(bf)

    def put(ref):
        ref[0, 0:half, :] = total.astype(bf)
        ref[0, half : half + GATE_ROWS, :] = jnp.zeros((GATE_ROWS, width), bf)
        ref[0, half : half + GATE_ROWS, 0:half] = placed

    @pl.when(step < 4)
    def _():
        put(mine_ref)
        out_mine_ref[0] = result.astype(bf)

    @pl.when(step >= 4)
    def _():
        put(other_ref)
        out_other_ref[0] = result.astype(bf)


def expert_pass(e, pieces, raw_all, wgu, wdown):
    rows, width = pieces[0].shape
    half = rows - GATE_ROWS
    hidden_units = wgu.shape[3]
    flops = 8 * half * width * hidden_units * 2 * 4
    return pl.pallas_call(
        ffn_kernel,
        out_shape=(
            jax.ShapeDtypeStruct((8, half, width), bf),
            jax.ShapeDtypeStruct((8, half, 2 * hidden_units), bf),
            jax.ShapeDtypeStruct((8, half, hidden_units), bf),
            jax.ShapeDtypeStruct((4, rows, width), bf),
            jax.ShapeDtypeStruct((4, rows, width), bf),
            jax.ShapeDtypeStruct((4, half, width), bf),
            jax.ShapeDtypeStruct((4, half, width), bf),
        ),
        grid_spec=pltpu.PrefetchScalarGridSpec(
            num_scalar_prefetch=1,
            grid=(8,),
            in_specs=[
                pl.BlockSpec((1, half, hidden_units), lambda i, e: (i, 0, 0)),
                pl.BlockSpec((1, 2, width, hidden_units), lambda i, e: (e[0], 0, 0, 0)),
                pl.BlockSpec((1, hidden_units, width), lambda i, e: (e[0], 0, 0)),
            ]
            + [pl.BlockSpec((rows, width), lambda i, e: (0, 0))] * 8,
            out_specs=(
                pl.BlockSpec((1, half, width), lambda i, e: (i, 0, 0)),
                pl.BlockSpec((1, half, 2 * hidden_units), lambda i, e: (i, 0, 0)),
                pl.BlockSpec((1, half, hidden_units), lambda i, e: (i, 0, 0)),
                pl.BlockSpec((1, rows, width), lambda i, e: (jnp.minimum(i, 3), 0, 0)),
                pl.BlockSpec((1, rows, width), lambda i, e: (jnp.maximum(i - 4, 0), 0, 0)),
                pl.BlockSpec((1, half, width), lambda i, e: (jnp.minimum(i, 3), 0, 0)),
                pl.BlockSpec((1, half, width), lambda i, e: (jnp.maximum(i - 4, 0), 0, 0)),
            ),
            scratch_shapes=[pltpu.VMEM((rows, width), bf)],
        ),
        compiler_params=pltpu.CompilerParams(vmem_limit_bytes=48 << 20),
        cost_estimate=pl.CostEstimate(flops=flops, bytes_accessed=40 << 20, transcendentals=2 << 20),
        name="expert_pass",
    )(e, raw_all, wgu, wdown, *pieces)


def hidden_cotangent_kernel(at_ref, w_ref, rows_ref, up_ref, raw_ref):
    rows = rows_ref[0]
    up_ref[0] = rows
    raw_ref[0] = dotf(rows, w_ref[0], 1, 1).astype(bf)


def hidden_cotangent(at, rows, w_down):
    pieces, half, width = rows.shape
    hidden_units = w_down.shape[1]
    return pl.pallas_call(
        hidden_cotangent_kernel,
        out_shape=(
            jax.ShapeDtypeStruct((pieces, half, width), bf),
            jax.ShapeDtypeStruct((pieces, half, hidden_units), bf),
        ),
        grid_spec=pltpu.PrefetchScalarGridSpec(
            num_scalar_prefetch=1,
            grid=(pieces,),
            in_specs=[
                pl.BlockSpec((1, hidden_units, width), lambda i, at: (at[0], 0, 0)),
                pl.BlockSpec((1, half, width), lambda i, at: (at[1 + i], 0, 0)),
            ],
            out_specs=(
                pl.BlockSpec((1, half, width), lambda i, at: (i, 0, 0)),
                pl.BlockSpec((1, half, hidden_units), lambda i, at: (i, 0, 0)),
            ),
        ),
        compiler_params=pltpu.CompilerParams(vmem_limit_bytes=40 << 20),
        cost_estimate=pl.CostEstimate(flops=32 * 10**8, bytes_accessed=12 << 20, transcendentals=0),
        name="hidden_cotangent",
    )(at, w_down, rows)


def exact(a, b, ca, cb):
    return lax.dot_general(a, b, (((ca,), (cb,)), ((), ())), precision=HIGHEST, preferred_element_type=f32)


def back_rows_kernel(
    first_ref, p0, p1, p2, p3, residual_ref, up_ref, gain_ref, rows_ref, small_ref, const_ref, own_ref, other_ref,
    grad_ref, low_ref, cot_ref, logit_ref, gain_out_ref,
):
    half, width = residual_ref.shape
    dx = p0[...].astype(f32) + p1[...].astype(f32) + p2[...].astype(f32) + p3[...].astype(f32)
    gating = dx[half : half + E_ALL, 0:half]
    dx = dx[0:half]
    residual, gain = residual_ref[...], gain_ref[...]
    up = up_ref[...].astype(f32)
    inverse = lax.rsqrt(jnp.mean(residual * residual, axis=-1, keepdims=True) + EPSILON)
    probs, hot = rows_ref[0:8], rows_ref[8:16]
    blend_one, blend_two, const_weight = rows_ref[16:18], rows_ref[18:20], rows_ref[20:22]
    kept = rows_ref[22:23]
    copy_dot = exact(jnp.ones((8, width), f32), up * (residual * inverse * gain), 1, 1)[0:1]
    vector_dot = exact(const_ref[...], up, 1, 1)[0:NCONST]
    const_dot = blend_one * copy_dot + blend_two * vector_dot
    row = lax.broadcasted_iota(jnp.int32, (8, half), 0)
    dots = jnp.where(row < E_FFN, gating, 0.0)
    dots = jnp.where(row == E_FFN + 1, copy_dot, dots)
    for c in range(NCONST):
        dots = jnp.where(row == E_FFN + 2 + c, const_dot[c : c + 1], dots)
    probs_grad = dots * hot
    logit_ref[0:8] = probs * (probs_grad - jnp.sum(probs * probs_grad, axis=0, keepdims=True))
    grad_one = const_weight * copy_dot
    grad_two = const_weight * vector_dot
    inner = blend_one * grad_one + blend_two * grad_two
    grad_one = blend_one * (grad_one - inner)
    grad_two = blend_two * (grad_two - inner)
    const_grad = jnp.zeros((8, half), f32)
    for c in range(NCONST):
        const_grad = jnp.where(row == 2 * c, grad_one[c : c + 1], const_grad)
        const_grad = jnp.where(row == 2 * c + 1, grad_two[c : c + 1], const_grad)
    logit_ref[8:16] = const_grad
    kept_column = jnp.broadcast_to(kept, (8, half)).T[:, 0:1]
    normed_grad = dx + exact(logit_ref[...], small_ref[...], 0, 0) + kept_column * up
    gain_out_ref[...] = jnp.sum(normed_grad * residual * inverse, axis=0, keepdims=True)
    scaled = normed_grad * gain
    mean = jnp.mean(scaled * residual, axis=-1, keepdims=True)
    grad = up + inverse * scaled - residual * (inverse * inverse * inverse * mean)
    grad_ref[...] = grad
    low = grad.astype(bf)
    low_ref[...] = low
    heads = own_ref.shape[0] // HD
    cot_ref[...] = jnp.zeros(cot_ref.shape, bf)
    for n, ref in enumerate((own_ref, other_ref)):
        rows = dotf(ref[...], low, 1, 1).astype(bf)
        for h in range(heads):
            cot_ref[first_ref[n] + h] = rows[h * HD : (h + 1) * HD]


def back_rows(first, parts, residual, up, gain, rows, small, const, own, other):
    half, width = residual.shape
    v = pl.BlockSpec(memory_space=pltpu.VMEM)
    return pl.pallas_call(
        back_rows_kernel,
        out_shape=(
            jax.ShapeDtypeStruct((half, width), f32),
            jax.ShapeDtypeStruct((half, width), bf),
            jax.ShapeDtypeStruct((SPAN, HD, half), bf),
            jax.ShapeDtypeStruct((16, half), f32),
            jax.ShapeDtypeStruct((1, width), f32),
        ),
        in_specs=[pl.BlockSpec(memory_space=pltpu.SMEM)] + [v] * 12,
        out_specs=(v,) * 5,
        compiler_params=pltpu.CompilerParams(vmem_limit_bytes=60 << 20),
        cost_estimate=pl.CostEstimate(flops=4 * 10**8, bytes_accessed=5 << 20, transcendentals=0),
        name="back_rows",
    )(first, *parts, residual, up, gain.reshape(1, width), rows, small, const, own, other)


def token_rows_kernel(first_ref, arrived_ref, own_ref, other_ref, grad_ref, x_ref, gain_ref, whole_ref, out_ref, rows):
    heads = own_ref.shape[2] // HD
    upstream = jnp.zeros(out_ref.shape, f32)
    for n, ref in enumerate((own_ref, other_ref)):
        for s in range(3):
            for h in range(heads):
                rows[h * HD : (h + 1) * HD, :] = arrived_ref[first_ref[n] + h, s * HD : (s + 1) * HD, :]
            upstream = upstream + dotf(rows[...], ref[s], 0, 1)
    x = x_ref[...].astype(f32)
    inverse = lax.rsqrt(jnp.mean(x * x, axis=-1, keepdims=True) + EPSILON)
    scaled = upstream * gain_ref[...]
    mean = jnp.mean(scaled * x, axis=-1, keepdims=True)
    out = grad_ref[...] + inverse * scaled - x * (inverse * inverse * inverse * mean)
    out_ref[...] = out
    whole_ref[pl.ds(pl.multiple_of(first_ref[2], out.shape[0]), out.shape[0]), :] = out


def token_rows(first, arrived, own, other, grad, x, gain):
    half, width = x.shape
    v = pl.BlockSpec(memory_space=pltpu.VMEM)
    return pl.pallas_call(
        token_rows_kernel,
        out_shape=(jax.ShapeDtypeStruct((2 * half, width), f32), jax.ShapeDtypeStruct((half, width), f32)),
        in_specs=[pl.BlockSpec(memory_space=pltpu.SMEM)] + [v] * 6,
        out_specs=(v, v),
        scratch_shapes=[pltpu.VMEM((own.shape[2], half), bf)],
        compiler_params=pltpu.CompilerParams(vmem_limit_bytes=60 << 20),
        cost_estimate=pl.CostEstimate(flops=10**9, bytes_accessed=6 << 20, transcendentals=0),
        name="token_rows",
    )(first, arrived, own, other, grad, x, gain.reshape(1, width))


def heads_kernel(first_ref, x_ref, gain_ref, w_ref, cos_ref, sin_ref, *refs):
    buffer_ref, normed_ref = refs[-2:]
    x = x_ref[...].astype(f32)
    inverse = lax.rsqrt(jnp.mean(x * x, axis=-1, keepdims=True) + EPSILON)
    normed = (x * inverse * gain_ref[...]).astype(bf)
    normed_ref[...] = normed
    cosine, sine = cos_ref[...], sin_ref[...]
    heads = w_ref.shape[2] // HD
    first = first_ref[0]
    buffer_ref[...] = refs[0][...] if len(refs) == 3 else jnp.zeros(buffer_ref.shape, bf)
    for s in range(3):
        rows = dotf(normed, w_ref[s], 1, 0).T
        for h in range(heads):
            part = rows[h * HD : (h + 1) * HD]
            if s < 2:
                one, two = part[: HD // 2], part[HD // 2 :]
                part = jnp.concatenate([one * cosine - two * sine, two * cosine + one * sine], axis=0)
            buffer_ref[first + h, s * HD : (s + 1) * HD, :] = part.astype(bf)


def head_rows(first, x, gain, w, cosine, sine, buffer=None):
    half, width = x.shape
    v = pl.BlockSpec(memory_space=pltpu.VMEM)
    given = [] if buffer is None else [buffer]
    return pl.pallas_call(
        heads_kernel,
        out_shape=(
            jax.ShapeDtypeStruct((SPAN, 3 * HD, half), bf),
            jax.ShapeDtypeStruct((half, width), bf),
        ),
        in_specs=[pl.BlockSpec(memory_space=pltpu.SMEM)] + [v] * 5 + [v] * len(given),
        out_specs=(v, v),
        compiler_params=pltpu.CompilerParams(vmem_limit_bytes=40 << 20),
        cost_estimate=pl.CostEstimate(flops=5 * 10**8, bytes_accessed=4 << 20, transcendentals=0),
        name="head_rows",
    )(first, x, gain.reshape(1, width), w, cosine, sine, *given)


def head_grad_kernel(at_ref, dq_ref, own_ref, other_ref, cos_ref, sin_ref, w_ref, *refs):
    pieces, out_ref, turned_rows = refs[:-2], refs[-2], refs[-1]
    half, width = pieces[0].shape[-2:]
    blocks = out_ref.shape[0]

    def back(rows, block):
        one, two = rows[: HD // 2], rows[HD // 2 :]
        cosine, sine = cos_ref[block], sin_ref[block]
        return jnp.concatenate([one * cosine + two * sine, two * cosine - one * sine], axis=0)

    acc = jnp.zeros((3 * HD, width), f32)
    n = 0
    for ref in pieces:
        places = list(np.ndindex(*ref.shape[:-2]))
        for k in range(len(places)):
            block = at_ref[n]
            dkv = own_ref[block] + other_ref[block].astype(f32)
            rows = jnp.concatenate(
                [back(dq_ref[block].astype(f32), block), back(dkv[:HD], block), dkv[HD:]], axis=0
            ).astype(bf)
            out_ref[block, 0 : 3 * HD, :] = rows
            turned_rows[:, k * half : (k + 1) * half] = rows
            n += 1
        count = len(places) * half
        acc = acc + dotf(turned_rows[:, 0:count], ref[...].reshape(count, width), 1, 0)
    gain_row = jnp.sum(acc * w_ref[...].astype(f32), axis=0, keepdims=True)
    turned = jnp.concatenate([acc, jnp.broadcast_to(gain_row, (8, width))], axis=0).T.astype(bf)
    rows = turned.shape[0] // blocks
    for block in range(blocks):
        out_ref[block, 3 * HD :, :] = jnp.zeros((rows, out_ref.shape[2]), bf)
        out_ref[block, 3 * HD :, 0 : 3 * HD + 8] = turned[block * rows : (block + 1) * rows]


def head_grad(at, dq, own, other, cosine, sine, w_head, pieces):
    v = pl.BlockSpec(memory_space=pltpu.VMEM)
    half, width = pieces[0].shape[-2:]
    blocks = dq.shape[0]
    return pl.pallas_call(
        head_grad_kernel,
        out_shape=jax.ShapeDtypeStruct((blocks, 3 * HD + width // blocks, half), bf),
        in_specs=[pl.BlockSpec(memory_space=pltpu.SMEM)] + [v] * (6 + len(pieces)),
        out_specs=v,
        scratch_shapes=[pltpu.VMEM((3 * HD, 4 * half), bf)],
        compiler_params=pltpu.CompilerParams(vmem_limit_bytes=60 << 20),
        cost_estimate=pl.CostEstimate(flops=12 * 10**8, bytes_accessed=12 << 20, transcendentals=0),
        name="head_grad",
    )(at, dq, own, other, cosine, sine, w_head, *pieces)


def finish_kernel(e_ref, *refs):
    parts, (gu_ref, down_ref, sum_ref) = refs[:4], refs[4:]
    units = down_ref.shape[1]
    rest = 3 * units
    rows = [p[...].astype(f32) for p in parts]
    sum_ref[...] = rows[0][:, rest:] + rows[1][:, rest:] + rows[2][:, rest:] + rows[3][:, rest:]
    for k in range(E_FFN):
        distance = e_ref[0] ^ k
        low = jnp.where(distance == 0, rows[0][:, :rest], rows[1][:, :rest])
        high = jnp.where(distance == 2, rows[2][:, :rest], rows[3][:, :rest])
        one = jnp.where(distance < 2, low, high)
        gu_ref[k, 0] = one[:, 0:units]
        gu_ref[k, 1] = one[:, units : 2 * units]
        down_ref[k] = one[:, 2 * units :].T


def finish(e, parts, units):
    slab, columns = parts[0].shape
    v = pl.BlockSpec(memory_space=pltpu.VMEM)
    return pl.pallas_call(
        finish_kernel,
        out_shape=(
            jax.ShapeDtypeStruct((E_FFN, 2, slab, units), f32),
            jax.ShapeDtypeStruct((E_FFN, units, slab), f32),
            jax.ShapeDtypeStruct((slab, columns - 3 * units), f32),
        ),
        in_specs=[pl.BlockSpec(memory_space=pltpu.SMEM)] + [v] * 4,
        out_specs=(v, v, v),
        compiler_params=pltpu.CompilerParams(vmem_limit_bytes=40 << 20),
        cost_estimate=pl.CostEstimate(flops=10**5, bytes_accessed=10**5, transcendentals=0),
        name="finish",
    )(e, *parts)


def swap(value, axis):
    return lax.ppermute(value, axis, [(0, 1), (1, 0)])


def plane_diagonal(value):
    return lax.ppermute(value, ("y", "x"), [(i, 3 - i) for i in range(4)])


def plane_gather(piece):
    mine = [piece, swap(piece, "x"), swap(piece, "y"), plane_diagonal(piece)]
    return mine + [swap(p, "t") for p in mine]


def plane_scatter(mine, other, later):
    held = [(mine[k].astype(f32) + other[k].astype(f32)).astype(bf) for k in range(4)]
    held, later = lax.optimization_barrier((held, later))
    return [held[0], swap(held[1], "x"), swap(held[2], "y"), plane_diagonal(held[3])], later


def over_z(value, distance):
    return lax.ppermute(value, "z", [(i, i ^ distance) for i in range(4)])


def total(parts):
    first, rest = parts
    return first.astype(f32) + sum(p.astype(f32) for p in rest)


def plane_rows(chunks):
    b = lax.axis_index(("y", "x"))
    pick = lambda d: lax.dynamic_index_in_dim(chunks, b ^ d, 0, keepdims=False)
    return pick(0), [swap(pick(1), "x"), swap(pick(2), "y"), plane_diagonal(pick(3))]


def after(value, *others):
    return lax.optimization_barrier((value, others))[0]


def over_sequences(rows):
    if lax.axis_size("s") == 1:
        return rows
    return lax.psum_scatter(rows, "s", scatter_dimension=0, tiled=True)


def first_tokens(segments):
    def gathered(value, moved, places):
        low, high = places
        first = jnp.where(low == 0, jnp.stack([value, moved[0]]), jnp.stack([moved[0], value]))
        second = jnp.where(low == 0, jnp.stack([moved[1], moved[2]]), jnp.stack([moved[2], moved[1]]))
        return jnp.where(high == 0, jnp.stack([first, second]), jnp.stack([second, first]))

    z = lax.axis_index("z")
    plane = [swap(segments, "x"), swap(segments, "y"), plane_diagonal(segments)]
    ids = gathered(segments, plane, (lax.axis_index("x"), lax.axis_index("y"))).reshape(-1)
    ids = gathered(ids, [over_z(ids, d) for d in (1, 2, 3)], (z % 2, z // 2)).reshape(-1)
    count = ids.shape[0]
    index = jnp.arange(count, dtype=jnp.int32)
    before = jnp.concatenate([ids[:1], ids[:-1]])
    opens = jnp.where(ids != before, index, 0).reshape(-1, 256)
    n = opens.shape[0]
    lane = jnp.arange(256, dtype=jnp.int32)
    within = jnp.max(jnp.where(lane[None, None, :] <= lane[None, :, None], opens[:, None, :], 0), axis=-1)
    block = jnp.arange(n, dtype=jnp.int32)
    top = jnp.max(opens, axis=1)
    carry = jnp.max(jnp.where(block[None, :] < block[:, None], top[None, :], 0), axis=1)
    return jnp.maximum(within, carry[:, None]).reshape(-1)


def rotary_tables(position, half_dim):
    inv_freq = jnp.exp(jnp.arange(half_dim).astype(f32) * (-math.log(10000.0) / half_dim))
    phases = inv_freq[:, None] * position.astype(f32)[None, :]
    return jnp.cos(phases), jnp.sin(phases)


def rotate(values, cosine, sine):
    half_dim = values.shape[-2] // 2
    one, two = values[..., :half_dim, :], values[..., half_dim:, :]
    return jnp.concatenate([one * cosine - two * sine, two * cosine + one * sine], axis=-2)


def norm_forward(values, gain):
    inverse = lax.rsqrt(jnp.mean(values * values, axis=-1, keepdims=True) + EPSILON)
    return values * inverse * gain, inverse


def norm_backward(values, inverse, gain, upstream):
    scaled = upstream * gain
    inner = jnp.mean(scaled * values, axis=-1, keepdims=True)
    return (
        inverse * scaled - values * inverse * inverse * inverse * inner,
        jnp.sum(upstream * values * inverse, axis=0),
    )


def local(
    tokens,
    segments,
    routes,
    prev_logits,
    attn_gain,
    w_qkv,
    w_out,
    ffn_gain,
    w_router,
    w_const,
    v_const,
    w_gu,
    w_down,
    cotangent,
):
    tok_count, width = tokens.shape
    half = tok_count // 2
    features = w_qkv.shape[2]
    heads = features // HD
    t = lax.axis_index("t")
    place = lax.axis_index(GROUP)
    expert = lax.axis_index(("y", "x"))

    def mine(value):
        return lax.dynamic_slice_in_dim(value, t * half, half, 0)

    def both_halves(value):
        other = swap(value, "t")
        whole = jnp.zeros((tok_count,) + value.shape[1:], value.dtype)
        whole = lax.dynamic_update_slice_in_dim(whole, value, t * half, 0)
        return lax.dynamic_update_slice_in_dim(whole, other, (1 - t) * half, 0)

    w_qkv_other = swap(w_qkv, "t")
    w_out_other = swap(w_out, "t")
    inputs = mine(tokens).astype(f32)
    upstream_low = mine(cotangent)
    upstream = upstream_low.astype(f32)
    my_routes = jnp.transpose(mine(routes))
    my_prev = jnp.transpose(mine(prev_logits))
    kinds = jnp.arange(E_ALL, dtype=jnp.int32)[:, None]
    hot = (my_routes[0:1] == kinds).astype(f32) + (my_routes[1:2] == kinds).astype(f32)
    position = (place * tok_count + t * half + jnp.arange(half, dtype=jnp.int32)) % SEQ_LEN
    cosine, sine = rotary_tables(position, HD // 2)
    tokens_mine = mine(tokens)
    first = (t * heads).astype(jnp.int32).reshape(1)
    other_first = ((1 - t) * heads).astype(jnp.int32).reshape(1)
    buffer, normed_low = head_rows(first, tokens_mine, attn_gain, w_qkv, cosine, sine)
    buffer, _ = head_rows(other_first, tokens_mine, attn_gain, w_qkv_other, cosine, sine, buffer)

    def of_heads(buffer):
        return (
            lax.dynamic_slice_in_dim(buffer, t * heads, heads, 0),
            lax.dynamic_slice_in_dim(buffer, (1 - t) * heads, heads, 0),
        )

    def exchange(buffer):
        return lax.all_to_all(buffer, GROUP, 0, 0, tiled=True)

    upstream_sent, segments, buffer = lax.optimization_barrier((upstream_low, segments, buffer))
    start_all = first_tokens(segments)
    sc, start_rows = bounds(start_all, t, SPAN, half)
    own = exchange(buffer)
    oth = swap(own[:, HD:], "t")
    up_gathered = lax.all_gather(upstream_sent, ("y", "x", "t"))
    piece_rank = jnp.bitwise_xor(2 * expert + t, jnp.array((0, 2, 4, 6, 1, 3, 5, 7), jnp.int32))
    expert_at = expert.astype(jnp.int32).reshape(1)
    normed_sent, own_q, sc, start_rows = lax.optimization_barrier((normed_low, own, sc, start_rows))
    along_z = [normed_sent] + [over_z(normed_sent, d) for d in (1, 2, 3)]
    heads_rows, heads_full, lse = flash_fwd(sc, start_rows, own_q, oth)
    heads_rows, up_gathered, along_z = lax.optimization_barrier((heads_rows, up_gathered, along_z))
    back = exchange(heads_rows)
    up_all, raw_all = hidden_cotangent(
        jnp.concatenate([expert_at, piece_rank.astype(jnp.int32)]), up_gathered, w_down
    )
    back, raw_all = lax.optimization_barrier((back, raw_all))
    heads_own, heads_other = (v.reshape(features, half) for v in of_heads(back))
    branch = dotf(heads_own, w_out, 0, 0) + dotf(heads_other, w_out_other, 0, 0)
    residual = inputs + branch
    normed_ffn, inverse_ffn = norm_forward(residual, ffn_gain)
    ffn_low = normed_ffn.astype(bf)
    w_small = jnp.concatenate([w_router, w_const], axis=1)
    logits = dotf(w_small, ffn_low, 0, 1)
    router_probs = jax.nn.softmax(logits[:E_ALL] + my_prev, axis=0)
    expert_weight = router_probs * hot
    gate_rows = expert_weight[:E_FFN]
    gate_high = gate_rows.astype(bf)
    gate_low = (gate_rows - gate_high.astype(f32)).astype(bf)
    gate_block = jnp.pad(
        jnp.concatenate([gate_high, gate_low]), ((0, GATE_ROWS - 2 * E_FFN), (0, width - half))
    )
    x_all = plane_gather(jnp.concatenate([ffn_low, gate_block]))
    w_held, w_other_held, t_late = after((w_qkv, w_qkv_other, t), ffn_low)
    all_position = (jnp.arange(SPAN, dtype=jnp.int32)[:, None] * tok_count + t_late * half)[:, :, None] + jnp.arange(half, dtype=jnp.int32)
    all_cosine, all_sine = rotary_tables(all_position.reshape(-1), HD // 2)
    by_block = lambda table: jnp.transpose(table.reshape(HD // 2, SPAN, half), (1, 0, 2))
    all_cosine, all_sine = by_block(all_cosine), by_block(all_sine)
    pair_a, pair_b = jnp.stack(along_z[:2]), jnp.stack(along_z[2:])
    near = (0, 4, 8, 12, 1, 5, 10, 14, 2, 6, 3, 7, 9, 13, 11, 15)
    at = jnp.bitwise_xor(place, jnp.array(near, jnp.int32)).astype(jnp.int32)
    head_first = jnp.minimum(place, 2 * heads - 1) % heads * HD
    of_head = lambda w: lax.dynamic_slice_in_dim(w, head_first, HD, 2)
    w_head = jnp.where(jnp.minimum(place // heads, 1) == t, of_head(w_held), of_head(w_other_held))
    w_head = jnp.swapaxes(w_head, 1, 2).reshape(3 * HD, width)
    x_all, all_cosine, all_sine, pair_a, pair_b, at, w_head = lax.optimization_barrier(
        (x_all, all_cosine, all_sine, pair_a, pair_b, at, w_head)
    )
    pair_ax, pair_by = swap(pair_a, "x"), swap(pair_b, "y")
    x_only, g_all, weighted, dx_mine, dx_other, out_mine, out_beside = expert_pass(
        expert_at, x_all, raw_all, w_gu, w_down
    )
    dx_mine, dx_other, pair_ax, pair_by = lax.optimization_barrier((dx_mine, dx_other, pair_ax, pair_by))
    dx_other = swap(dx_other, "t")
    hidden_units = w_down.shape[1]
    received, (weighted, g_all) = plane_scatter(dx_mine, dx_other, (weighted, g_all))
    down_part = jnp.einsum("ptd,ptf->df", up_all, weighted, preferred_element_type=f32).astype(bf)
    gu_part = jnp.einsum("ptd,ptf->df", x_only, g_all, preferred_element_type=f32).astype(bf)
    expert_part = over_sequences(jnp.concatenate([gu_part, down_part], axis=1))
    slab = expert_part.shape[0] // SPAN
    received, expert_part = lax.optimization_barrier((received, expert_part))
    expert_sum = lax.psum_scatter(expert_part, "z", scatter_dimension=0, tiled=True)

    pairs = logits[E_ALL:].reshape(NCONST, 2, half)
    blend_one = jax.nn.sigmoid(pairs[:, 0] - pairs[:, 1])
    blend_two = jax.nn.sigmoid(pairs[:, 1] - pairs[:, 0])
    const_weight = expert_weight[E_FFN + 2 :]
    kept = expert_weight[E_FFN + 1 : E_FFN + 2] + jnp.sum(const_weight * blend_one, axis=0, keepdims=True)
    added = const_weight * blend_two
    columns = jnp.transpose(jnp.concatenate([kept, added]))
    kept_column, added_columns = columns[:, 0:1], columns[:, 1:]

    pad_rows = lambda v, n: jnp.pad(v, ((0, n - v.shape[0]), (0, 0)))
    row_pack = pad_rows(jnp.concatenate([router_probs, hot, blend_one, blend_two, const_weight, kept]), 24)
    small_rows = pad_rows(jnp.transpose(w_small).astype(f32), 16)
    residual_grad, branch_cot, cot, logit_grad, ffn_gain_part = back_rows(
        jnp.concatenate([first, other_first]),
        received,
        residual,
        upstream_low,
        ffn_gain,
        row_pack,
        small_rows,
        pad_rows(v_const, 8),
        w_out,
        w_out_other,
    )
    logit_grad = logit_grad[: E_ALL + 2 * NCONST]
    prev_grad = logit_grad[:E_ALL]
    out_beside, added = after((out_beside, added), cot)
    small = jnp.concatenate(
        [
            ffn_gain_part,
            jnp.dot(logit_grad, ffn_low.astype(f32), precision=HIGHEST),
            jnp.dot(added, upstream, precision=HIGHEST),
        ]
    )
    small = jnp.transpose(jnp.pad(small, ((0, 128 - small.shape[0]), (0, 0)))).astype(bf)
    out_own = dotf(branch_cot, heads_own, 0, 1).astype(bf)
    out_other = dotf(branch_cot, heads_other, 0, 1).astype(bf)
    out_part = (out_own.astype(f32) + swap(out_other, "t").astype(f32)).astype(bf)
    out_part = over_sequences(jnp.concatenate([out_part, small], axis=1))
    out_z = lax.psum_scatter(out_part, "z", scatter_dimension=0, tiled=True)
    out_beside = swap(out_beside, "t")
    held = [(out_mine[k].astype(f32) + out_beside[k].astype(f32)).astype(bf) for k in range(4)]

    cot = exchange(cot)
    stack_a, stack_b = jnp.stack([pair_a, pair_ax]), jnp.stack([pair_b, pair_by])
    cot, held, out_part, stack_a, stack_b = lax.optimization_barrier((cot, held, out_part, stack_a, stack_b))
    pair_ya, pair_xb = swap(stack_a, "y"), swap(stack_b, "x")
    moved_out = [swap(held[1], "x"), swap(held[2], "y"), plane_diagonal(held[3])]
    dq, dkv_own, dkv_oth = flash_bwd(sc, start_rows, own, oth, cot, heads_full, lse)
    dkv_oth, pair_ya, pair_xb, moved_out = lax.optimization_barrier((dkv_oth, pair_ya, pair_xb, moved_out))
    dkv_oth = swap(dkv_oth, "t")
    sent = head_grad(
        at, dq, dkv_own, dkv_oth, all_cosine, all_sine, w_head, [pair_a, pair_b, pair_ax, pair_by, pair_ya, pair_xb]
    )
    if lax.axis_size("s") > 1:
        head_part = over_sequences(sent[:, 3 * HD :].reshape(width, half))
        sent = jnp.concatenate([sent[:, : 3 * HD], head_part.reshape(SPAN, slab, half)], axis=1)
    sent, held, expert_sum, out_z, prev_grad = lax.optimization_barrier((sent, held, expert_sum, out_z, prev_grad))
    arrived = exchange(sent)
    d_first = (lax.axis_index("s") * SPAN + place) * slab

    prev_both = both_halves(jnp.transpose(prev_grad))
    parts = jnp.concatenate([expert_sum, out_z], axis=1)
    own_rows, got_rows = plane_rows(parts.reshape(4, slab, parts.shape[1]))
    held, moved_out = after((held, moved_out), parts)
    ffn_sum = sum(v.astype(f32) for v in [held[0]] + moved_out)
    mixture = residual + ffn_sum + kept_column * normed_ffn + jnp.dot(added_columns, v_const, precision=HIGHEST)
    output = both_halves(mixture.astype(bf))
    w_gu_grad, w_down_grad, out_done = finish(expert_at, [own_rows] + got_rows, hidden_units)
    token_at = jnp.concatenate([first, other_first, (t * half).astype(jnp.int32).reshape(1)])
    arrived, prev_both, output, w_gu_grad, w_down_grad, out_done, token_at = lax.optimization_barrier(
        (arrived, prev_both, output, w_gu_grad, w_down_grad, out_done, token_at)
    )
    w_out_grad = jnp.transpose(out_done[:, :features])
    small = out_done[:, features:]
    small = small + swap(small, "t")
    arrived_own, arrived_other = of_heads(arrived)
    part_own, part_other = arrived_own[:, 3 * HD :, : 3 * HD], arrived_other[:, 3 * HD :, : 3 * HD]
    head_sum = part_own.astype(f32) + swap(part_other, "t").astype(f32)
    w_qkv_grad = jnp.transpose(head_sum.reshape(heads, slab, 3, HD), (2, 1, 0, 3)).reshape(3, slab, features)
    gain_part = jnp.sum(arrived[: 2 * heads, 3 * HD :, 3 * HD].astype(f32), axis=0)
    attn_gain_grad = (gain_part + swap(gain_part, "t")) / lax.dynamic_slice_in_dim(attn_gain, d_first, slab, 0)

    tokens_grad, grad_half = token_rows(
        token_at, arrived, w_qkv, w_qkv_other, residual_grad, tokens_mine, attn_gain
    )
    tokens_grad = lax.dynamic_update_slice_in_dim(tokens_grad, swap(grad_half, "t"), (1 - t) * half, 0)
    return (
        output,
        tokens_grad,
        prev_both,
        attn_gain_grad,
        w_qkv_grad,
        w_out_grad,
        small[:, 0],
        small[:, 1 : 1 + E_ALL],
        small[:, 9 : 9 + 2 * NCONST],
        jnp.transpose(small[:, 13 : 13 + NCONST]),
        w_gu_grad,
        w_down_grad,
    )


def solution(mesh):
    dp = mesh.shape["dp"]
    devices = mesh.devices.reshape(dp // SPAN, 4, 2, 2, mesh.shape["tensor"])
    inner = Mesh(devices, ("s", "z", "y", "x", "t"))
    d = ("s", "z", "y", "x")
    return jax.shard_map(
        local,
        mesh=inner,
        in_specs=(
            P(d, None),
            P(d),
            P(d, None),
            P(d, None),
            P(),
            P(None, None, "t"),
            P("t", None),
            P(),
            P(),
            P(),
            P(),
            P(None, None, None, "t"),
            P(None, "t", None),
            P(d, None),
        ),
        out_specs=(
            P(d, None),
            P(d, None),
            P(d, None),
            P(d),
            P(None, d, "t"),
            P("t", d),
            P(d),
            P(d, None),
            P(d, None),
            P(None, d),
            P(None, None, d, "t"),
            P(None, "t", d),
        ),
        check_vma=False,
    )
```

profile of v0, /device:TPU:17, one launch (start us, length us, event | category | flops | bytes accessed | tf_op | source)
XLA Modules:
  0.0 431.7 jit_solution(12744710477374357575)
XLA Ops:
  9.0 1.5 copy-done.4
  12.4 3.6 head_rows.3
  16.1 6.6 %all-to-all-start = ((bf16[16,192,256]{2,1,0:T(8,128)(2,1)}), bf16[16,192,256]{2,1,0:T(8,128)(2,1)S(1)}, u32[]{:S(2)}, u32[]{:S(2)}) async-start(bf16[16,192,256]{2,1,0:T(8,128)(2,1)} %get-tuple-element.121), calls=%async_computation | async-start | bytes 3145728 | tf_op jit(solution)/shard_map/all_to_all | solution.py:773
  23.6 1.2 collective-permute-start.2
  26.3 4.6 %collective-permute-done.2 = s32[512]{0:T(512)S(1)} collective-permute-done((s32[512]{0:T(512)S(1)}, s32[512]{0:T(512)S(1)}, u32[]{:S(2)}, u32[]{:S(2)}) %collective-permute-start.2) | collective-permute-done | bytes 2080 | tf_op jit(solution)/shard_map/ppermute | solution.py:623
  31.0 5.0 %collective-permute-start.4 = (s32[2048]{0:T(1024)S(1)}, s32[2048]{0:T(1024)S(1)}, u32[]{:S(2)}, u32[]{:S(2)}) collective-permute-start(s32[2048]{0:T(1024)S(1)} %bitcast.126), channel_id=1, source_target_pairs={{0,8},{8,0},{16,24},{24,16},{1,9},{9,1},{17,25},{25,17},{2,10},{10... | collective-permute-start | bytes 24584 | tf_op jit(solution)/shard_map/ppermute | solution.py:642
  36.0 1.3 collective-permute-start.6
  37.3 12.6 %collective-permute-done.4 = s32[2048]{0:T(1024)S(1)} collective-permute-done((s32[2048]{0:T(1024)S(1)}, s32[2048]{0:T(1024)S(1)}, u32[]{:S(2)}, u32[]{:S(2)}) %collective-permute-start.4) | collective-permute-done | bytes 8224 | tf_op jit(solution)/shard_map/ppermute | solution.py:642
  49.9 6.8 %collective-permute-done.5 = s32[2048]{0:T(1024)S(1)} collective-permute-done((s32[2048]{0:T(1024)S(1)}, s32[2048]{0:T(1024)S(1)}, u32[]{:S(2)}, u32[]{:S(2)}) %collective-permute-start.5) | collective-permute-done | bytes 8224 | tf_op jit(solution)/shard_map/ppermute | solution.py:642
  56.8 1.4 collective-permute-done.6
  59.6 1.2 select_reduce_fusion
  62.3 1.3 collective-permute-start.7
  65.4 2.0 collective-permute-start.8
  67.6 41.4 %flash_fwd.1 = (bf16[16,64,256]{2,1,0:T(8,128)(2,1)}, f32[16,64,256]{2,1,0:T(8,128)S(1)}, f32[16,1,256]{2,1,0:T(1,128)S(1)}) custom-call(s32[65]{0:T(128)S(1)} %concatenate.103.sc, s32[16,1,256]{2,1,0:T(1,128)S(1)} %dynamic-slice_maximum_fusion.start_ref, bf16[16,192,256]{2,1,0:T(8,128)(2,1)S(1)} %all-to-all-done.own_ref, ...), custom_call_target="tpu_custom_call" | custom-call | flops 1000000000 | bytes 4194304 | tf_op jit(solution)/shard_map/flash_fwd/pallas_call | solution.py:119
  112.1 7.0 %all-to-all-start.1 = ((bf16[16,64,256]{2,1,0:T(8,128)(2,1)}), bf16[16,64,256]{2,1,0:T(8,128)(2,1)S(1)}, u32[]{:S(2)}, u32[]{:S(2)}) async-start(bf16[16,64,256]{2,1,0:T(8,128)(2,1)} %get-tuple-element.129), calls=%async_computation.1 | async-start | bytes 1048576 | tf_op jit(solution)/shard_map/all_to_all | solution.py:773
  120.3 1.9 copy-done.12
  122.2 6.9 %hidden_cotangent.1 = (bf16[8,256,768]{2,1,0:T(8,128)(2,1)S(1)}, bf16[8,256,1024]{2,1,0:T(8,128)(2,1)S(1)}) custom-call(s32[9]{0:T(128)S(1)} %pad_add_fusion.1.at_ref, bf16[4,1024,768]{2,1,0:T(8,128)(2,1)} %wd_ref.1, bf16[8,256,768]{2,1,0:T(8,128)(2,1)S(1)} %bitcast.111), custom_call_target="tpu_custom_call" | custom-call | flops 3200000000 | bytes 12582912 | tf_op jit(solution)/shard_map/hidden_cotangent/pallas_call | solution.py:370
  129.1 2.1 copy-done.15
  131.2 1.6 copy-done.16
  132.9 1.6 fusion.35
  134.5 1.6 multiply_reduce_fusion
  137.0 1.2 collective-permute-start.12
  138.3 1.2 collective-permute-start.13
  140.7 2.0 pad_maximum_fusion.4.refs_1_
  142.7 1.5 collective-permute-start.15
  144.1 1.6 select_bitcast_fusion
  147.6 2.6 collective-permute-start.16
  150.3 9.0 %collective-permute-start.17 = (bf16[272,768]{1,0:T(8,128)(2,1)S(1)}, bf16[272,768]{1,0:T(8,128)(2,1)S(1)}, u32[]{:S(2)}, u32[]{:S(2)}) collective-permute-start(bf16[272,768]{1,0:T(8,128)(2,1)S(1)} %collective-permute-done.13.refs_2_), channel_id=1, source_target_pairs={{0,1},{1,0},{2,3},{3,2},{4,5},{5,4},{6,7},{7,6},{8,9},{9,8},{10,11... | collective-permute-start | bytes 1253384 | tf_op jit(solution)/shard_map/ppermute | solution.py:623
  159.4 2.8 multiply_sine_fusion
  164.8 25.1 %expert_pass.1 = (bf16[8,256,768]{2,1,0:T(8,128)(2,1)}, bf16[8,256,2048]{2,1,0:T(8,128)(2,1)}, bf16[8,256,1024]{2,1,0:T(8,128)(2,1)}, bf16[4,272,768]{2,1,0:T(8,...) custom-call(s32[1]{0:T(128)} %bitcast.11.e_ref, ...), custom_call_target="tpu_custom_call" | custom-call | flops 12884901888 | bytes 41943040 | tf_op jit(solution)/shard_map/expert_pass/pallas_call | solution.py:324
  194.3 3.0 fusion.8
  197.3 1.2 collective-permute-start.22
  199.9 9.6 %bitcast_convert_fusion = bf16[768,2048]{1,0:T(8,128)(2,1)S(1)} fusion(bf16[8,256,768]{2,1,0:T(8,128)(2,1)S(1)} %copy-done.60, bf16[8,256,2048]{2,1,0:T(8,128)(2,1)} %get-tuple-element.163), kind=kOutput, calls=%fused_computation.1 | convolution fusion | flops 6444023808 | bytes 14680064 | tf_op jit(solution)/shard_map/ptd,ptf->df/dot_general | solution.py:832
  209.5 3.5 bitcast_convert_fusion.1
  213.1 2.6 pad_maximum_fusion
  215.7 1.7 collective-permute-done.24.p3
  217.4 6.4 %back_rows.1 = (f32[256,768]{1,0:T(8,128)}, bf16[256,768]{1,0:T(8,128)(2,1)}, bf16[16,64,256]{2,1,0:T(8,128)(2,1)}, f32[16,256]{1,0:T(8,128)}, f32[1,768]{1,0:T(1,128)}) custom-call(s32[2]{0:T(128)} %pad_add_fusion.2.first_ref, bf16[272,768]{1,0:T(8,128)(2,1)} %get-tuple-element.166.p0, bf16[272,768]{1,0:T(8,128)(2,1)} %copy-done.34, ...), custom_call_target="tpu_custom_call" | custom-call | flops 400000000 | bytes 5242880 | tf_op jit(solution)/shard_map/back_rows/pallas_call | solution.py:452
  223.8 2.3 convolution_convert_fusion
  226.0 3.0 collective-permute-start.26
  233.6 4.9 %all-to-all-start.2 = ((bf16[16,64,256]{2,1,0:T(8,128)(2,1)}), bf16[16,64,256]{2,1,0:T(8,128)(2,1)S(1)}, u32[]{:S(2)}, u32[]{:S(2)}) async-start(bf16[16,64,256]{2,1,0:T(8,128)(2,1)} %get-tuple-element.170), calls=%async_computation.2 | async-start | bytes 1048576 | tf_op jit(solution)/shard_map/all_to_all | solution.py:773
  238.5 2.7 pad_maximum_fusion.2
  241.2 2.8 pad_maximum_fusion.1
  244.0 2.5 fusion.12
  246.5 16.6 %all-to-all-done.2.do_ref = bf16[16,64,256]{2,1,0:T(8,128)(2,1)S(1)} async-done(((bf16[16,64,256]{2,1,0:T(8,128)(2,1)}), bf16[16,64,256]{2,1,0:T(8,128)(2,1)S(1)}, u32[]{:S(2)}, u32[]{:S(2)}) %all-to-all-start.2) | async-done | bytes 524320 | tf_op jit(solution)/shard_map/all_to_all | solution.py:773
  264.6 1.5 collective-permute-start.30
  266.9 73.6 %flash_bwd.1 = (bf16[16,64,256]{2,1,0:T(8,128)(2,1)}, f32[16,128,256]{2,1,0:T(8,128)}, bf16[16,128,256]{2,1,0:T(8,128)(2,1)}) custom-call(s32[65]{0:T(128)} %copy-done.11, s32[16,1,256]{2,1,0:T(1,128)} %copy-done.8, bf16[16,192,256]{2,1,0:T(8,128)(2,1)} %copy-done.2, bf16[16,128,256]{2,1,0:T(8,128)(2,1)} %copy-done.5, bf16[16,64,256]{2,1,0:T(8,128)(2,1)} %copy-done.23, ...), custom_call_target="tpu_custom_call" | custom-call | flops 1000000000 | bytes 4194304 | tf_op jit(solution)/shard_map/flash_bwd/pallas_call | solution.py:225
  341.3 2.9 collective-permute-done.32.other_ref
  345.2 7.2 %head_grad.1 = bf16[16,240,256]{2,1,0:T(8,128)(2,1)} custom-call(s32[16]{0:T(128)} %broadcast_xor_fusion.at_ref, bf16[16,64,256]{2,1,0:T(8,128)(2,1)} %get-tuple-element.183.dq_ref, f32[16,128,256]{2,1,0:T(8,128)} %get-tuple-element.184.own_ref, bf16[16,128,256]{2,1,0:T(8,128)(2,1)} %copy-done.32, f32[16,32,256]{2,1,0:T(8,128)} %get-tuple-element.192.cos_ref, ...), custom_call_target="tpu_custom_call" | custom-call | flops 1200000000 | bytes 12582912 | tf_op jit(solution)/shard_map/head_grad/pallas_call | solution.py:576
  352.4 5.9 %all-to-all-start.3 = ((bf16[16,240,256]{2,1,0:T(8,128)(2,1)}), bf16[16,240,256]{2,1,0:T(8,128)(2,1)}, u32[]{:S(2)}, u32[]{:S(2)}) async-start(bf16[16,240,256]{2,1,0:T(8,128)(2,1)} %head_grad.1), calls=%async_computation.5 | async-start | bytes 3932160 | tf_op jit(solution)/shard_map/all_to_all | solution.py:773
  359.5 1.2 collective-permute-start.35
  360.7 1.2 collective-permute-start.36
  362.3 1.9 constant_dynamic-update-slice_fusion.6
  365.0 1.6 collective-permute-start.34
  368.4 4.5 %collective-permute-done.35.refs_1_ = bf16[48,3584]{1,0:T(8,128)(2,1)S(1)} collective-permute-done((bf16[48,3584]{1,0:T(8,128)(2,1)S(1)}, bf16[48,3584]{1,0:T(8,128)(2,1)S(1)}, u32[]{:S(2)}, u32[]{:S(2)}) %collective-permute-start.35) | collective-permute-done | bytes 344096 | tf_op jit(solution)/shard_map/ppermute | solution.py:623
  372.8 17.2 %collective-permute-done.36.refs_2_ = bf16[48,3584]{1,0:T(8,128)(2,1)S(1)} collective-permute-done((bf16[48,3584]{1,0:T(8,128)(2,1)S(1)}, bf16[48,3584]{1,0:T(8,128)(2,1)S(1)}, u32[]{:S(2)}, u32[]{:S(2)}) %collective-permute-start.36) | collective-permute-done | bytes 344096 | tf_op jit(solution)/shard_map/ppermute | solution.py:623
  390.0 6.3 %collective-permute-done.37.refs_3_ = bf16[48,3584]{1,0:T(8,128)(2,1)S(1)} collective-permute-done((bf16[48,3584]{1,0:T(8,128)(2,1)S(1)}, bf16[48,3584]{1,0:T(8,128)(2,1)S(1)}, u32[]{:S(2)}, u32[]{:S(2)}) %collective-permute-start.37) | collective-permute-done | bytes 344096 | tf_op jit(solution)/shard_map/ppermute | solution.py:627
  396.3 1.8 finish.1
  398.8 1.8 constant_dynamic-update-slice_fusion.5
  400.6 2.8 all-to-all-done.3.arrived_ref
  404.0 1.5 slice_bitcast_fusion
  405.6 1.3 collective-permute-start.41
  409.5 5.9 %token_rows.1 = (f32[512,768]{1,0:T(8,128)}, f32[256,768]{1,0:T(8,128)}) custom-call(s32[3]{0:T(128)} %pad_add_fusion.3.first_ref, bf16[16,240,256]{2,1,0:T(8,128)(2,1)} %all-to-all-done.3.arrived_ref, bf16[3,768,384]{2,1,0:T(8,128)(2,1)} %own_ref.3, bf16[3,768,384]{2,1,0:T(8,128)(2,1)} %collective-permute-done.w_ref.other_ref, ...), custom_call_target="tpu_custom_call" | custom-call | flops 1000000000 | bytes 6291456 | tf_op jit(solution)/shard_map/token_rows/pallas_call | solution.py:489
  415.4 1.5 copy.90
  416.9 1.3 dynamic-slice_divide_fusion
  (292 shorter events, 51.1 us)
Async XLA Ops:
  7.2 104.9 %all-gather.3.cloned.1.call-start = ((), (), s32[]{:S(2)}) async-start(), calls=%async_computation.8 | async-start | bytes 3538944 | tf_op jit(solution)/shard_map/all_gather | solution.py:780
  7.2 5.1 %collective-permute-start = (bf16[3,768,384]{2,1,0:T(8,128)(2,1)}, bf16[3,768,384]{2,1,0:T(8,128)(2,1)}, u32[]{:S(2)}, u32[]{:S(2)}) collective-permute-start(bf16[3,768,384]{2,1,0:T(8,128)(2,1)} %own_ref.3), channel_id=1, source_target_pairs={{0,1},{1,0},{2,3},{3,2},{4,5},{5,4},{6,7},{7,6},{8,9},{9,8},{10,11... | collective-permute-start | bytes 5308424 | tf_op jit(solution)/shard_map/ppermute | solution.py:623
  8.8 125.7 %copy-start.3 = (bf16[256,768]{1,0:T(8,128)(2,1)}, bf16[256,768]{1,0:T(8,128)(2,1)S(1)}, u32[]{:S(2)}) copy-start(bf16[256,768]{1,0:T(8,128)(2,1)S(1)} %constant_dynamic-slice_fusion.6.x_ref) | copy-start | bytes 1179652
  16.1 45.1 %all-to-all-start = ((bf16[16,192,256]{2,1,0:T(8,128)(2,1)}), bf16[16,192,256]{2,1,0:T(8,128)(2,1)S(1)}, u32[]{:S(2)}, u32[]{:S(2)}) async-start(bf16[16,192,256]{2,1,0:T(8,128)(2,1)} %get-tuple-element.121), calls=%async_computation | async-start | bytes 3145728 | tf_op jit(solution)/shard_map/all_to_all | solution.py:773
  22.6 44.9 %copy-start.56 = (s32[512,2]{0,1:T(2,128)S(1)}, s32[512,2]{0,1:T(2,128)}, u32[]{:S(2)}) copy-start(s32[512,2]{0,1:T(2,128)} %param.18) | copy-start | bytes 12292
  22.6 44.9 %copy-start.58 = (s32[8]{0:T(128)S(1)}, s32[8]{0:T(128)}, u32[]{:S(2)}) copy-start(s32[8]{0:T(128)} %constant.158.clone) | copy-start | bytes 100
  22.6 111.8 %collective-permute-start.11 = (bf16[384,768]{1,0:T(8,128)(2,1)}, bf16[384,768]{1,0:T(8,128)(2,1)}, u32[]{:S(2)}, u32[]{:S(2)}) collective-permute-start(bf16[384,768]{1,0:T(8,128)(2,1)} %own_ref.2), channel_id=1, source_target_pairs={{0,1},{1,0},{2,3},{3,2},{4,5},{5,4},{6,7},{7,6},{8,9},{9,8},{10,11... | collective-permute-start | bytes 1769480 | tf_op jit(solution)/shard_map/ppermute | solution.py:623
  23.6 7.3 %collective-permute-start.2 = (s32[512]{0:T(512)S(1)}, s32[512]{0:T(512)S(1)}, u32[]{:S(2)}, u32[]{:S(2)}) collective-permute-start(s32[512]{0:T(512)S(1)} %copy-done.55), channel_id=1, source_target_pairs={{0,4},{4,0},{1,5},{5,1},{2,6},{6,2},{3,7},{7,3},{8,12},{12,8},{9,1... | collective-permute-start | bytes 6152 | tf_op jit(solution)/shard_map/ppermute | solution.py:623
  24.8 6.0 %collective-permute-start.3 = (s32[512]{0:T(512)S(1)}, s32[512]{0:T(512)S(1)}, u32[]{:S(2)}, u32[]{:S(2)}) collective-permute-start(s32[512]{0:T(512)S(1)} %copy-done.55), channel_id=1, source_target_pairs={{0,6},{2,4},{4,2},{6,0},{1,7},{3,5},{5,3},{7,1},{8,14},{10,12},{12... | collective-permute-start | bytes 6152 | tf_op jit(solution)/shard_map/ppermute | solution.py:627
  26.0 4.9 %collective-permute-start.1 = (s32[512]{0:T(512)S(1)}, s32[512]{0:T(512)S(1)}, u32[]{:S(2)}, u32[]{:S(2)}) collective-permute-start(s32[512]{0:T(512)S(1)} %copy-done.55), channel_id=1, source_target_pairs={{0,2},{2,0},{1,3},{3,1},{4,6},{6,4},{5,7},{7,5},{8,10},{10,8},{9,1... | collective-permute-start | bytes 6152 | tf_op jit(solution)/shard_map/ppermute | solution.py:623
  31.0 18.9 %collective-permute-start.4 = (s32[2048]{0:T(1024)S(1)}, s32[2048]{0:T(1024)S(1)}, u32[]{:S(2)}, u32[]{:S(2)}) collective-permute-start(s32[2048]{0:T(1024)S(1)} %bitcast.126), channel_id=1, source_target_pairs={{0,8},{8,0},{16,24},{24,16},{1,9},{9,1},{17,25},{25,17},{2,10},{10... | collective-permute-start | bytes 24584 | tf_op jit(solution)/shard_map/ppermute | solution.py:642
  36.0 20.7 %collective-permute-start.5 = (s32[2048]{0:T(1024)S(1)}, s32[2048]{0:T(1024)S(1)}, u32[]{:S(2)}, u32[]{:S(2)}) collective-permute-start(s32[2048]{0:T(1024)S(1)} %bitcast.127), channel_id=1, source_target_pairs={{0,16},{8,24},{16,0},{24,8},{1,17},{9,25},{17,1},{25,9},{2,18},{10... | collective-permute-start | bytes 24584 | tf_op jit(solution)/shard_map/ppermute | solution.py:642
  36.0 22.1 %collective-permute-start.6 = (s32[2048]{0:T(1024)S(1)}, s32[2048]{0:T(1024)S(1)}, u32[]{:S(2)}, u32[]{:S(2)}) collective-permute-start(s32[2048]{0:T(1024)S(1)} %bitcast.128), channel_id=1, source_target_pairs={{0,24},{8,16},{16,8},{24,0},{1,25},{9,17},{17,9},{25,1},{2,26},{10... | collective-permute-start | bytes 24584 | tf_op jit(solution)/shard_map/ppermute | solution.py:642
  61.2 47.8 %copy-start.2 = (bf16[16,192,256]{2,1,0:T(8,128)(2,1)}, bf16[16,192,256]{2,1,0:T(8,128)(2,1)S(1)}, u32[]{:S(2)}) copy-start(bf16[16,192,256]{2,1,0:T(8,128)(2,1)S(1)} %all-to-all-done.own_ref) | copy-start | bytes 4718596
  62.3 5.3 %collective-permute-start.7 = (bf16[16,128,256]{2,1,0:T(8,128)(2,1)}, bf16[16,128,256]{2,1,0:T(8,128)(2,1)S(1)}, u32[]{:S(2)}, u32[]{:S(2)}) collective-permute-start(bf16[16,128,256]{2,1,0:T(8,128)(2,1)} %slice.179), channel_id=1, source_target_pairs={{0,1},{1,0},{2,3},{3,2},{4,5},{5,4},{6,7},{7,6},{8,9},{9,8},{10,11... | collective-permute-start | bytes 3145736 | tf_op jit(solution)/shard_map/ppermute | solution.py:623
  63.7 45.3 %copy-start.8 = (s32[16,1,256]{2,1,0:T(1,128)}, s32[16,1,256]{2,1,0:T(1,128)S(1)}, u32[]{:S(2)}) copy-start(s32[16,1,256]{2,1,0:T(1,128)S(1)} %dynamic-slice_maximum_fusion.start_ref) | copy-start | bytes 49156
  64.3 44.6 %copy-start.11 = (s32[65]{0:T(128)}, s32[65]{0:T(128)S(1)}, u32[]{:S(2)}) copy-start(s32[65]{0:T(128)S(1)} %concatenate.103.sc) | copy-start | bytes 784
  64.3 46.2 %collective-permute-start.10 = (bf16[256,768]{1,0:T(8,128)(2,1)S(1)}, bf16[256,768]{1,0:T(8,128)(2,1)S(1)}, u32[]{:S(2)}, u32[]{:S(2)}) collective-permute-start(bf16[256,768]{1,0:T(8,128)(2,1)S(1)} %get-tuple-element.134), channel_id=1, source_target_pairs={{0,24},{8,16},{16,8},{24,0},{1,25},{9,17},{17,9},{25,1},{2,26},{10... | collective-permute-start | bytes 1179656 | tf_op jit(solution)/shard_map/ppermute | solution.py:642
  65.4 45.2 %collective-permute-start.8 = (bf16[256,768]{1,0:T(8,128)(2,1)S(1)}, bf16[256,768]{1,0:T(8,128)(2,1)S(1)}, u32[]{:S(2)}, u32[]{:S(2)}) collective-permute-start(bf16[256,768]{1,0:T(8,128)(2,1)S(1)} %get-tuple-element.134), channel_id=1, source_target_pairs={{0,8},{8,0},{16,24},{24,16},{1,9},{9,1},{17,25},{25,17},{2,10},{10... | collective-permute-start | bytes 1179656 | tf_op jit(solution)/shard_map/ppermute | solution.py:642
  67.4 44.7 %collective-permute-start.9 = (bf16[256,768]{1,0:T(8,128)(2,1)S(1)}, bf16[256,768]{1,0:T(8,128)(2,1)}, u32[]{:S(2)}, u32[]{:S(2)}) collective-permute-start(bf16[256,768]{1,0:T(8,128)(2,1)S(1)} %get-tuple-element.134), channel_id=1, source_target_pairs={{0,16},{8,24},{16,0},{24,8},{1,17},{9,25},{17,1},{25,9},{2,18},{10... | collective-permute-start | bytes 1179656 | tf_op jit(solution)/shard_map/ppermute | solution.py:642
  67.5 52.2 %copy-start.52 = (bf16[768,8]{0,1:T(8,128)(2,1)S(1)}, bf16[768,8]{0,1:T(8,128)(2,1)}, u32[]{:S(2)}) copy-start(bf16[768,8]{0,1:T(8,128)(2,1)} %param.24) | copy-start | bytes 36868
  67.6 52.2 %copy-start.53 = (bf16[768,4]{0,1:T(4,128)(2,1)S(1)}, bf16[768,4]{0,1:T(4,128)(2,1)}, u32[]{:S(2)}) copy-start(bf16[768,4]{0,1:T(4,128)(2,1)} %param.25) | copy-start | bytes 18436
  67.6 52.2 %copy-start.57 = (s32[16]{0:T(128)S(1)}, s32[16]{0:T(128)}, u32[]{:S(2)}) copy-start(s32[16]{0:T(128)} %constant.159.clone) | copy-start | bytes 196
  67.6 41.4 %copy-start.5 = (bf16[16,128,256]{2,1,0:T(8,128)(2,1)}, bf16[16,128,256]{2,1,0:T(8,128)(2,1)S(1)}, u32[]{:S(2)}) copy-start(bf16[16,128,256]{2,1,0:T(8,128)(2,1)S(1)} %collective-permute-done.7.oth_ref) | copy-start | bytes 3145732
  112.1 20.8 %all-to-all-start.1 = ((bf16[16,64,256]{2,1,0:T(8,128)(2,1)}), bf16[16,64,256]{2,1,0:T(8,128)(2,1)S(1)}, u32[]{:S(2)}, u32[]{:S(2)}) async-start(bf16[16,64,256]{2,1,0:T(8,128)(2,1)} %get-tuple-element.129), calls=%async_computation.1 | async-start | bytes 1048576 | tf_op jit(solution)/shard_map/all_to_all | solution.py:773
  119.1 233.3 %reduce-scatter.5.cloned.1.call-start = ((), (), s32[]{:S(2)}) async-start(), calls=%async_computation.7 | async-start | bytes 983040 | tf_op jit(solution)/shard_map/reduce_scatter | solution.py:877
  137.0 10.6 %collective-permute-start.12 = (bf16[272,768]{1,0:T(8,128)(2,1)S(1)}, bf16[272,768]{1,0:T(8,128)(2,1)S(1)}, u32[]{:S(2)}, u32[]{:S(2)}) collective-permute-start(bf16[272,768]{1,0:T(8,128)(2,1)S(1)} %pad_maximum_fusion.6.refs_0_), channel_id=1, source_target_pairs={{0,2},{2,0},{1,3},{3,1},{4,6},{6,4},{5,7},{7,5},{8,10},{10,8},{9,1... | collective-permute-start | bytes 1253384 | tf_op jit(solution)/shard_map/ppermute | solution.py:623
  138.3 12.0 %collective-permute-start.13 = (bf16[272,768]{1,0:T(8,128)(2,1)S(1)}, bf16[272,768]{1,0:T(8,128)(2,1)S(1)}, u32[]{:S(2)}, u32[]{:S(2)}) collective-permute-start(bf16[272,768]{1,0:T(8,128)(2,1)S(1)} %pad_maximum_fusion.6.refs_0_), channel_id=1, source_target_pairs={{0,4},{4,0},{1,5},{5,1},{2,6},{6,2},{3,7},{7,3},{8,12},{12,8},{9,1... | collective-permute-start | bytes 1253384 | tf_op jit(solution)/shard_map/ppermute | solution.py:623
  139.5 19.8 %collective-permute-start.14 = (bf16[272,768]{1,0:T(8,128)(2,1)S(1)}, bf16[272,768]{1,0:T(8,128)(2,1)S(1)}, u32[]{:S(2)}, u32[]{:S(2)}) collective-permute-start(bf16[272,768]{1,0:T(8,128)(2,1)S(1)} %pad_maximum_fusion.6.refs_0_), channel_id=1, source_target_pairs={{0,6},{2,4},{4,2},{6,0},{1,7},{3,5},{5,3},{7,1},{8,14},{10,12},{12... | collective-permute-start | bytes 1253384 | tf_op jit(solution)/shard_map/ppermute | solution.py:627
  142.7 19.5 %collective-permute-start.15 = (bf16[272,768]{1,0:T(8,128)(2,1)S(1)}, bf16[272,768]{1,0:T(8,128)(2,1)S(1)}, u32[]{:S(2)}, u32[]{:S(2)}) collective-permute-start(bf16[272,768]{1,0:T(8,128)(2,1)S(1)} %pad_maximum_fusion.6.refs_0_), channel_id=1, source_target_pairs={{0,1},{1,0},{2,3},{3,2},{4,5},{5,4},{6,7},{7,6},{8,9},{9,8},{10,11... | collective-permute-start | bytes 1253384 | tf_op jit(solution)/shard_map/ppermute | solution.py:623
  147.6 14.6 %collective-permute-start.16 = (bf16[272,768]{1,0:T(8,128)(2,1)S(1)}, bf16[272,768]{1,0:T(8,128)(2,1)S(1)}, u32[]{:S(2)}, u32[]{:S(2)}) collective-permute-start(bf16[272,768]{1,0:T(8,128)(2,1)S(1)} %collective-permute-done.12.refs_1_), channel_id=1, source_target_pairs={{0,1},{1,0},{2,3},{3,2},{4,5},{5,4},{6,7},{7,6},{8,9},{9,8},{10,11... | collective-permute-start | bytes 1253384 | tf_op jit(solution)/shard_map/ppermute | solution.py:623
  150.3 11.9 %collective-permute-start.17 = (bf16[272,768]{1,0:T(8,128)(2,1)S(1)}, bf16[272,768]{1,0:T(8,128)(2,1)S(1)}, u32[]{:S(2)}, u32[]{:S(2)}) collective-permute-start(bf16[272,768]{1,0:T(8,128)(2,1)S(1)} %collective-permute-done.13.refs_2_), channel_id=1, source_target_pairs={{0,1},{1,0},{2,3},{3,2},{4,5},{5,4},{6,7},{7,6},{8,9},{9,8},{10,11... | collective-permute-start | bytes 1253384 | tf_op jit(solution)/shard_map/ppermute | solution.py:623
  159.3 2.9 collective-permute-start.18
  162.2 27.6 %collective-permute-start.19 = (bf16[2,256,768]{2,1,0:T(8,128)(2,1)}, bf16[2,256,768]{2,1,0:T(8,128)(2,1)}, u32[]{:S(2)}, u32[]{:S(2)}) collective-permute-start(bf16[2,256,768]{2,1,0:T(8,128)(2,1)} %pad_maximum_fusion.3.refs_0_), channel_id=1, source_target_pairs={{0,2},{2,0},{1,3},{3,1},{4,6},{6,4},{5,7},{7,5},{8,10},{10,8},{9,1... | collective-permute-start | bytes 2359304 | tf_op jit(solution)/shard_map/ppermute | solution.py:623
  163.1 26.7 %collective-permute-start.20 = (bf16[2,256,768]{2,1,0:T(8,128)(2,1)}, bf16[2,256,768]{2,1,0:T(8,128)(2,1)}, u32[]{:S(2)}, u32[]{:S(2)}) collective-permute-start(bf16[2,256,768]{2,1,0:T(8,128)(2,1)} %pad_maximum_fusion.4.refs_1_), channel_id=1, source_target_pairs={{0,4},{4,0},{1,5},{5,1},{2,6},{6,2},{3,7},{7,3},{8,12},{12,8},{9,1... | collective-permute-start | bytes 2359304 | tf_op jit(solution)/shard_map/ppermute | solution.py:623
  164.8 26.7 %copy-start.50 = (f32[2,768]{1,0:T(2,128)S(1)}, f32[2,768]{1,0:T(2,128)}, u32[]{:S(2)}) copy-start(f32[2,768]{1,0:T(2,128)} %param.26) | copy-start | bytes 18436
  189.9 4.4 %collective-permute-start.21 = (bf16[4,272,768]{2,1,0:T(8,128)(2,1)}, bf16[4,272,768]{2,1,0:T(8,128)(2,1)S(1)}, u32[]{:S(2)}, u32[]{:S(2)}) collective-permute-start(bf16[4,272,768]{2,1,0:T(8,128)(2,1)} %get-tuple-element.155), channel_id=1, source_target_pairs={{0,1},{1,0},{2,3},{3,2},{4,5},{5,4},{6,7},{7,6},{8,9},{9,8},{10,11... | collective-permute-start | bytes 5013512 | tf_op jit(solution)/shard_map/ppermute | solution.py:623
  197.3 18.4 %collective-permute-start.22 = (bf16[272,768]{1,0:T(8,128)(2,1)}, bf16[272,768]{1,0:T(8,128)(2,1)S(1)}, u32[]{:S(2)}, u32[]{:S(2)}) collective-permute-start(bf16[272,768]{1,0:T(8,128)(2,1)} %get-tuple-element.159), channel_id=1, source_target_pairs={{0,2},{2,0},{1,3},{3,1},{4,6},{6,4},{5,7},{7,5},{8,10},{10,8},{9,1... | collective-permute-start | bytes 1253384 | tf_op jit(solution)/shard_map/ppermute | solution.py:623
  198.5 17.2 %collective-permute-start.23 = (bf16[272,768]{1,0:T(8,128)(2,1)}, bf16[272,768]{1,0:T(8,128)(2,1)S(1)}, u32[]{:S(2)}, u32[]{:S(2)}) collective-permute-start(bf16[272,768]{1,0:T(8,128)(2,1)} %get-tuple-element.160), channel_id=1, source_target_pairs={{0,4},{4,0},{1,5},{5,1},{2,6},{6,2},{3,7},{7,3},{8,12},{12,8},{9,1... | collective-permute-start | bytes 1253384 | tf_op jit(solution)/shard_map/ppermute | solution.py:623
  198.7 18.6 %collective-permute-start.24 = (bf16[272,768]{1,0:T(8,128)(2,1)}, bf16[272,768]{1,0:T(8,128)(2,1)}, u32[]{:S(2)}, u32[]{:S(2)}) collective-permute-start(bf16[272,768]{1,0:T(8,128)(2,1)} %get-tuple-element.161), channel_id=1, source_target_pairs={{0,6},{2,4},{4,2},{6,0},{1,7},{3,5},{5,3},{7,1},{8,14},{10,12},{12... | collective-permute-start | bytes 1253384 | tf_op jit(solution)/shard_map/ppermute | solution.py:627
  215.6 14.1 %copy-start.20 = (bf16[256,768]{1,0:T(8,128)(2,1)S(1)}, bf16[256,768]{1,0:T(8,128)(2,1)}, u32[]{:S(2)}) copy-start(bf16[256,768]{1,0:T(8,128)(2,1)} %constant_dynamic-slice_fusion.5.up_ref) | copy-start | bytes 1179652
  215.6 14.4 %copy-start.22 = (bf16[256,768]{1,0:T(8,128)(2,1)S(1)}, bf16[256,768]{1,0:T(8,128)(2,1)}, u32[]{:S(2)}) copy-start(bf16[256,768]{1,0:T(8,128)(2,1)} %copy-done.21) | copy-start | bytes 1179652
  226.0 5.3 %collective-permute-start.26 = (bf16[768,384]{1,0:T(8,128)(2,1)}, bf16[768,384]{1,0:T(8,128)(2,1)S(1)}, u32[]{:S(2)}, u32[]{:S(2)}) collective-permute-start(bf16[768,384]{1,0:T(8,128)(2,1)} %convolution_convert_fusion), channel_id=1, source_target_pairs={{0,1},{1,0},{2,3},{3,2},{4,5},{5,4},{6,7},{7,6},{8,9},{9,8},{10,11... | collective-permute-start | bytes 1769480 | tf_op jit(solution)/shard_map/ppermute | solution.py:623
  232.8 119.6 %reduce-scatter.3.cloned.1.call-start = ((), (), s32[]{:S(2)}) async-start(), calls=%async_computation.6 | async-start | bytes 5898240 | tf_op jit(solution)/shard_map/reduce_scatter | solution.py:836
  233.5 10.5 %collective-permute-start.25 = (bf16[4,256,768]{2,1,0:T(8,128)(2,1)}, bf16[4,256,768]{2,1,0:T(8,128)(2,1)}, u32[]{:S(2)}, u32[]{:S(2)}) collective-permute-start(bf16[4,256,768]{2,1,0:T(8,128)(2,1)} %get-tuple-element.173), channel_id=1, source_target_pairs={{0,1},{1,0},{2,3},{3,2},{4,5},{5,4},{6,7},{7,6},{8,9},{9,8},{10,11... | collective-permute-start | bytes 4718600 | tf_op jit(solution)/shard_map/ppermute | solution.py:623
  233.6 29.5 %all-to-all-start.2 = ((bf16[16,64,256]{2,1,0:T(8,128)(2,1)}), bf16[16,64,256]{2,1,0:T(8,128)(2,1)S(1)}, u32[]{:S(2)}, u32[]{:S(2)}) async-start(bf16[16,64,256]{2,1,0:T(8,128)(2,1)} %get-tuple-element.170), calls=%async_computation.2 | async-start | bytes 1048576 | tf_op jit(solution)/shard_map/all_to_all | solution.py:773
  263.1 77.5 %collective-permute-start.27 = (bf16[2,2,256,768]{3,2,1,0:T(8,128)(2,1)}, bf16[2,2,256,768]{3,2,1,0:T(8,128)(2,1)S(1)}, u32[]{:S(2)}, u32[]{:S(2)}) collective-permute-start(bf16[2,2,256,768]{3,2,1,0:T(8,128)(2,1)} %pad_maximum_fusion.1), channel_id=1, source_target_pairs={{0,4},{4,0},{1,5},{5,1},{2,6},{6,2},{3,7},{7,3},{8,12},{12,8},{9,1... | collective-permute-start | bytes 4718600 | tf_op jit(solution)/shard_map/ppermute | solution.py:623
  263.1 77.5 %collective-permute-start.28 = (bf16[2,2,256,768]{3,2,1,0:T(8,128)(2,1)}, bf16[2,2,256,768]{3,2,1,0:T(8,128)(2,1)}, u32[]{:S(2)}, u32[]{:S(2)}) collective-permute-start(bf16[2,2,256,768]{3,2,1,0:T(8,128)(2,1)} %pad_maximum_fusion.2), channel_id=1, source_target_pairs={{0,2},{2,0},{1,3},{3,1},{4,6},{6,4},{5,7},{7,5},{8,10},{10,8},{9,1... | collective-permute-start | bytes 4718600 | tf_op jit(solution)/shard_map/ppermute | solution.py:623
  264.3 76.3 %collective-permute-start.29 = (bf16[256,768]{1,0:T(8,128)(2,1)S(1)}, bf16[256,768]{1,0:T(8,128)(2,1)S(1)}, u32[]{:S(2)}, u32[]{:S(2)}) collective-permute-start(bf16[256,768]{1,0:T(8,128)(2,1)S(1)} %get-tuple-element.188), channel_id=1, source_target_pairs={{0,2},{2,0},{1,3},{3,1},{4,6},{6,4},{5,7},{7,5},{8,10},{10,8},{9,1... | collective-permute-start | bytes 1179656 | tf_op jit(solution)/shard_map/ppermute | solution.py:623
  264.6 76.0 %collective-permute-start.30 = (bf16[256,768]{1,0:T(8,128)(2,1)S(1)}, bf16[256,768]{1,0:T(8,128)(2,1)S(1)}, u32[]{:S(2)}, u32[]{:S(2)}) collective-permute-start(bf16[256,768]{1,0:T(8,128)(2,1)S(1)} %get-tuple-element.189), channel_id=1, source_target_pairs={{0,4},{4,0},{1,5},{5,1},{2,6},{6,2},{3,7},{7,3},{8,12},{12,8},{9,1... | collective-permute-start | bytes 1179656 | tf_op jit(solution)/shard_map/ppermute | solution.py:623
  266.0 74.5 %collective-permute-start.31 = (bf16[256,768]{1,0:T(8,128)(2,1)S(1)}, bf16[256,768]{1,0:T(8,128)(2,1)S(1)}, u32[]{:S(2)}, u32[]{:S(2)}) collective-permute-start(bf16[256,768]{1,0:T(8,128)(2,1)S(1)} %get-tuple-element.190), channel_id=1, source_target_pairs={{0,6},{2,4},{4,2},{6,0},{1,7},{3,5},{5,3},{7,1},{8,14},{10,12},{12... | collective-permute-start | bytes 1179656 | tf_op jit(solution)/shard_map/ppermute | solution.py:627
  266.9 74.4 %copy-start.49 = (f32[16,256]{1,0:T(8,128)S(1)}, f32[16,256]{1,0:T(8,128)}, u32[]{:S(2)}) copy-start(f32[16,256]{1,0:T(8,128)} %get-tuple-element.176) | copy-start | bytes 49156
  341.3 2.9 collective-permute-start.32
  352.4 50.9 %all-to-all-start.3 = ((bf16[16,240,256]{2,1,0:T(8,128)(2,1)}), bf16[16,240,256]{2,1,0:T(8,128)(2,1)}, u32[]{:S(2)}, u32[]{:S(2)}) async-start(bf16[16,240,256]{2,1,0:T(8,128)(2,1)} %head_grad.1), calls=%async_computation.5 | async-start | bytes 3932160 | tf_op jit(solution)/shard_map/all_to_all | solution.py:773
  359.5 13.3 %collective-permute-start.35 = (bf16[48,3584]{1,0:T(8,128)(2,1)S(1)}, bf16[48,3584]{1,0:T(8,128)(2,1)S(1)}, u32[]{:S(2)}, u32[]{:S(2)}) collective-permute-start(bf16[48,3584]{1,0:T(8,128)(2,1)S(1)} %get-tuple-element.308), channel_id=1, source_target_pairs={{0,2},{2,0},{1,3},{3,1},{4,6},{6,4},{5,7},{7,5},{8,10},{10,8},{9,1... | collective-permute-start | bytes 1032200 | tf_op jit(solution)/shard_map/ppermute | solution.py:623
  360.7 29.3 %collective-permute-start.36 = (bf16[48,3584]{1,0:T(8,128)(2,1)S(1)}, bf16[48,3584]{1,0:T(8,128)(2,1)S(1)}, u32[]{:S(2)}, u32[]{:S(2)}) collective-permute-start(bf16[48,3584]{1,0:T(8,128)(2,1)S(1)} %get-tuple-element.307), channel_id=1, source_target_pairs={{0,4},{4,0},{1,5},{5,1},{2,6},{6,2},{3,7},{7,3},{8,12},{12,8},{9,1... | collective-permute-start | bytes 1032200 | tf_op jit(solution)/shard_map/ppermute | solution.py:623
  361.9 34.4 %collective-permute-start.37 = (bf16[48,3584]{1,0:T(8,128)(2,1)S(1)}, bf16[48,3584]{1,0:T(8,128)(2,1)S(1)}, u32[]{:S(2)}, u32[]{:S(2)}) collective-permute-start(bf16[48,3584]{1,0:T(8,128)(2,1)S(1)} %get-tuple-element.306), channel_id=1, source_target_pairs={{0,6},{2,4},{4,2},{6,0},{1,7},{3,5},{5,3},{7,1},{8,14},{10,12},{12... | collective-permute-start | bytes 1032200 | tf_op jit(solution)/shard_map/ppermute | solution.py:627
  365.0 33.7 %collective-permute-start.34 = (bf16[256,768]{1,0:T(8,128)(2,1)}, bf16[256,768]{1,0:T(8,128)(2,1)}, u32[]{:S(2)}, u32[]{:S(2)}) collective-permute-start(bf16[256,768]{1,0:T(8,128)(2,1)} %get-tuple-element.327), channel_id=1, source_target_pairs={{0,1},{1,0},{2,3},{3,2},{4,5},{5,4},{6,7},{7,6},{8,9},{9,8},{10,11... | collective-permute-start | bytes 1179656 | tf_op jit(solution)/shard_map/ppermute | solution.py:623
  367.2 1.2 collective-permute-start.33
  368.4 47.0 %copy-start.51 = (f32[512,8]{0,1:T(8,128)}, f32[512,8]{0,1:T(8,128)S(1)}, u32[]{:S(2)}) copy-start(f32[512,8]{0,1:T(8,128)S(1)} %constant_dynamic-update-slice_fusion.7) | copy-start | bytes 49156
  405.6 12.6 %collective-permute-start.41 = (f32[48,128]{1,0:T(8,128)S(1)}, f32[48,128]{1,0:T(8,128)S(1)}, u32[]{:S(2)}, u32[]{:S(2)}) collective-permute-start(f32[48,128]{1,0:T(8,128)S(1)} %slice.170), channel_id=1, source_target_pairs={{0,1},{1,0},{2,3},{3,2},{4,5},{5,4},{6,7},{7,6},{8,9},{9,8},{10,11... | collective-permute-start | bytes 73736 | tf_op jit(solution)/shard_map/ppermute | solution.py:623
  408.9 12.8 %collective-permute-start.40 = (bf16[6,48,192]{2,1,0:T(8,128)(2,1)S(1)}, bf16[6,48,192]{2,1,0:T(8,128)(2,1)S(1)}, u32[]{:S(2)}, u32[]{:S(2)}) collective-permute-start(bf16[6,48,192]{2,1,0:T(8,128)(2,1)S(1)} %constant_dynamic-slice_fusion), channel_id=1, source_target_pairs={{0,1},{1,0},{2,3},{3,2},{4,5},{5,4},{6,7},{7,6},{8,9},{9,8},{10,11... | collective-permute-start | bytes 331784 | tf_op jit(solution)/shard_map/ppermute | solution.py:623
  409.0 7.9 %collective-permute-start.39 = (f32[48]{0:T(128)S(1)}, f32[48]{0:T(128)S(1)}, u32[]{:S(2)}, u32[]{:S(2)}) collective-permute-start(f32[48]{0:T(128)S(1)} %convert_reduce_fusion), channel_id=1, source_target_pairs={{0,1},{1,0},{2,3},{3,2},{4,5},{5,4},{6,7},{7,6},{8,9},{9,8},{10,11... | collective-permute-start | bytes 584 | tf_op jit(solution)/shard_map/ppermute | solution.py:623
  415.3 8.7 %collective-permute-start.38 = (f32[256,768]{1,0:T(8,128)}, f32[256,768]{1,0:T(8,128)S(1)}, u32[]{:S(2)}, u32[]{:S(2)}) collective-permute-start(f32[256,768]{1,0:T(8,128)} %get-tuple-element.219), channel_id=1, source_target_pairs={{0,1},{1,0},{2,3},{3,2},{4,5},{5,4},{6,7},{7,6},{8,9},{9,8},{10,11... | collective-permute-start | bytes 2359304 | tf_op jit(solution)/shard_map/ppermute | solution.py:623
  (46 other events, 149.5 us)
Sparse Core Ops, SparseCore 0:
  16.2 50.0 all-gather.2
  232.9 30.2 reduce-scatter.4
  265.5 85.8 reduce-scatter.2
where the time goes:
time: 440 us; the launch traced here: 432 us
  Pallas kernels  173 us (39%)
  waiting for transfers between devices  80.4 us (18%)
  starting transfers between devices  74.5 us (17%)
  local copies, waits for them, and re-layouts  34.2 us (8%)
  other arithmetic  32.4 us (7%)
  matrix products  22.3 us (5%)
  between operations  15.1 us (3%)
    pallas_call x1, Pallas kernels, flash_bwd(): pl.pallas_call(functools.partial(bwd_kernel, nb, half, j0, j1), out_shape...  73.6 us
    pallas_call x1, Pallas kernels, flash_fwd(): pl.pallas_call(functools.partial(fwd_kernel, nb, half), out_shape=(jax.Sh...  41.4 us
    ppermute x31, starting transfers between devices, swap(): return lax.ppermute(value, axis, [(0, 1), (1, 0)])  36.1 us
    ppermute x31, waiting for transfers between devices, swap(): return lax.ppermute(value, axis, [(0, 1), (1, 0)])  31.5 us
    pallas_call x1, Pallas kernels, expert_pass(): pl.pallas_call(ffn_kernel, out_shape=(jax.ShapeDtypeStruct((8, half, widt...  25.1 us
    all_to_all x4, starting transfers between devices, exchange(): return lax.all_to_all(buffer, GROUP, 0, 0, tiled=True)  24.4 us
    ppermute x6, waiting for transfers between devices, over_z(): return lax.ppermute(value, 'z', [(i, i ^ distance) for i in range(4)])  20.8 us
    all_to_all x4, waiting for transfers between devices, exchange(): return lax.all_to_all(buffer, GROUP, 0, 0, tiled=True)  19.4 us
  transfers between devices with their start and end apart: 49, of which 14 were waited for; matrix products, arithmetic and copies ran while one was open for 14% of the time, Pallas kernels for 38%

commit v1 on v0

--- a/solution.py
+++ b/solution.py
@@ -85,7 +85,7 @@
         c = (jnp.zeros((1, half), f32), jnp.zeros((HD, half), f32))
         c = plain(s, 1, c, True)
         for masked, first, end in ((True, lo, ml), (False, jnp.maximum(lo, ml), s)):
-            for n in WIDE:
+            for n in (8,) + WIDE:
                 count = jnp.maximum(end - first, 0) // n
                 c = lax.fori_loop(0, count, lambda i, c: plain(first + i * n, n, c, masked), c)
                 first = first + count * n
@@ -905,8 +905,8 @@
     output = both_halves(mixture.astype(bf))
     w_gu_grad, w_down_grad, out_done = finish(expert_at, [own_rows] + got_rows, hidden_units)
     token_at = jnp.concatenate([first, other_first, (t * half).astype(jnp.int32).reshape(1)])
-    arrived, prev_both, output, w_gu_grad, w_down_grad, out_done, token_at = lax.optimization_barrier(
-        (arrived, prev_both, output, w_gu_grad, w_down_grad, out_done, token_at)
+    arrived, prev_both, w_gu_grad, w_down_grad, out_done, token_at = lax.optimization_barrier(
+        (arrived, prev_both, w_gu_grad, w_down_grad, out_done, token_at)
     )
     w_out_grad = jnp.transpose(out_done[:, :features])
     small = out_done[:, features:]

time: 440 us -> 434 us (0.986)
  Pallas kernels: 173 us -> 159 us
  starting transfers between devices: 74.5 us -> 87.7 us
    ppermute x31, starting transfers between devices: 36.1 us -> 48.3 us  [swap(): return lax.ppermute(value, axis, [(0, 1), (1, 0)])]
    pallas_call x1, Pallas kernels: 73.6 us -> 64.8 us  [flash_bwd(): pl.pallas_call(functools.partial(bwd_kernel, nb, half, j0, j1), out_shape...]
    pallas_call x1, Pallas kernels: 41.4 us -> 36.3 us  [flash_fwd(): pl.pallas_call(functools.partial(fwd_kernel, nb, half), out_shape=(jax.Sh...]
  transfers between devices with their start and end apart: 49 -> 49, of which waited for: 14 -> 14; matrix products, arithmetic and copies ran while one was open for 14% -> 14% of each run, Pallas kernels for 38% -> 35%
where the time goes in v1:
time: 434 us; the launch traced here: 429 us
  Pallas kernels  159 us (37%)
  starting transfers between devices  87.7 us (20%)
  waiting for transfers between devices  78.6 us (18%)
  local copies, waits for them, and re-layouts  34.2 us (8%)
  other arithmetic  32.4 us (7%)
  matrix products  22.3 us (5%)
  between operations  15.1 us (3%)
    pallas_call x1, Pallas kernels, flash_bwd(): pl.pallas_call(functools.partial(bwd_kernel, nb, half, j0, j1), out_shape...  64.8 us
    ppermute x31, starting transfers between devices, swap(): return lax.ppermute(value, axis, [(0, 1), (1, 0)])  48.3 us
    pallas_call x1, Pallas kernels, flash_fwd(): pl.pallas_call(functools.partial(fwd_kernel, nb, half), out_shape=(jax.Sh...  36.3 us
    ppermute x31, waiting for transfers between devices, swap(): return lax.ppermute(value, axis, [(0, 1), (1, 0)])  29 us
    all_to_all x4, starting transfers between devices, exchange(): return lax.all_to_all(buffer, GROUP, 0, 0, tiled=True)  25.7 us
    pallas_call x1, Pallas kernels, expert_pass(): pl.pallas_call(ffn_kernel, out_shape=(jax.ShapeDtypeStruct((8, half, widt...  25.1 us
    ppermute x6, waiting for transfers between devices, over_z(): return lax.ppermute(value, 'z', [(i, i ^ distance) for i in range(4)])  20.2 us
    all_to_all x4, waiting for transfers between devices, exchange(): return lax.all_to_all(buffer, GROUP, 0, 0, tiled=True)  19.8 us
  transfers between devices with their start and end apart: 49, of which 14 were waited for; matrix products, arithmetic and copies ran while one was open for 14% of the time, Pallas kernels for 35%

profile of v1, /device:TPU:17, one launch (start us, length us, event | category | flops | bytes accessed | tf_op | source)
XLA Modules:
  0.0 429.3 jit_solution(1940481766608608067)
XLA Ops:
  9.0 1.5 copy-done.4
  12.4 3.6 head_rows.3
  16.1 7.2 %all-to-all-start = ((bf16[16,192,256]{2,1,0:T(8,128)(2,1)}), bf16[16,192,256]{2,1,0:T(8,128)(2,1)S(1)}, u32[]{:S(2)}, u32[]{:S(2)}) async-start(bf16[16,192,256]{2,1,0:T(8,128)(2,1)} %get-tuple-element.120), calls=%async_computation | async-start | bytes 3145728 | tf_op jit(solution)/shard_map/all_to_all | solution.py:773
  24.3 1.2 collective-permute-start.2
  27.0 4.1 collective-permute-done.2
  32.0 5.2 %collective-permute-start.4 = (s32[2048]{0:T(1024)S(1)}, s32[2048]{0:T(1024)S(1)}, u32[]{:S(2)}, u32[]{:S(2)}) collective-permute-start(s32[2048]{0:T(1024)S(1)} %bitcast.126), channel_id=1, source_target_pairs={{0,8},{8,0},{16,24},{24,16},{1,9},{9,1},{17,25},{25,17},{2,10},{10... | collective-permute-start | bytes 24584 | tf_op jit(solution)/shard_map/ppermute | solution.py:642
  37.2 1.3 collective-permute-start.6
  38.5 12.0 %collective-permute-done.4 = s32[2048]{0:T(1024)S(1)} collective-permute-done((s32[2048]{0:T(1024)S(1)}, s32[2048]{0:T(1024)S(1)}, u32[]{:S(2)}, u32[]{:S(2)}) %collective-permute-start.4) | collective-permute-done | bytes 8224 | tf_op jit(solution)/shard_map/ppermute | solution.py:642
  50.5 6.8 %collective-permute-done.5 = s32[2048]{0:T(1024)S(1)} collective-permute-done((s32[2048]{0:T(1024)S(1)}, s32[2048]{0:T(1024)S(1)}, u32[]{:S(2)}, u32[]{:S(2)}) %collective-permute-start.5) | collective-permute-done | bytes 8224 | tf_op jit(solution)/shard_map/ppermute | solution.py:642
  57.3 1.4 collective-permute-done.6
  60.2 1.2 select_reduce_fusion
  62.9 1.3 collective-permute-start.7
  66.0 2.0 collective-permute-start.8
  68.2 36.3 %flash_fwd.1 = (bf16[16,64,256]{2,1,0:T(8,128)(2,1)}, f32[16,64,256]{2,1,0:T(8,128)S(1)}, f32[16,1,256]{2,1,0:T(1,128)S(1)}) custom-call(s32[65]{0:T(128)S(1)} %concatenate.103.sc, s32[16,1,256]{2,1,0:T(1,128)S(1)} %dynamic-slice_maximum_fusion.start_ref, bf16[16,192,256]{2,1,0:T(8,128)(2,1)S(1)} %all-to-all-done.own_ref, ...), custom_call_target="tpu_custom_call" | custom-call | flops 1000000000 | bytes 4194304 | tf_op jit(solution)/shard_map/flash_fwd/pallas_call | solution.py:119
  107.5 6.8 %all-to-all-start.1 = ((bf16[16,64,256]{2,1,0:T(8,128)(2,1)}), bf16[16,64,256]{2,1,0:T(8,128)(2,1)S(1)}, u32[]{:S(2)}, u32[]{:S(2)}) async-start(bf16[16,64,256]{2,1,0:T(8,128)(2,1)} %get-tuple-element.128), calls=%async_computation.1 | async-start | bytes 1048576 | tf_op jit(solution)/shard_map/all_to_all | solution.py:773
  115.2 1.9 copy-done.12
  117.1 6.9 %hidden_cotangent.1 = (bf16[8,256,768]{2,1,0:T(8,128)(2,1)S(1)}, bf16[8,256,1024]{2,1,0:T(8,128)(2,1)S(1)}) custom-call(s32[9]{0:T(128)S(1)} %pad_add_fusion.1.at_ref, bf16[4,1024,768]{2,1,0:T(8,128)(2,1)} %wd_ref.1, bf16[8,256,768]{2,1,0:T(8,128)(2,1)S(1)} %bitcast.111), custom_call_target="tpu_custom_call" | custom-call | flops 3200000000 | bytes 12582912 | tf_op jit(solution)/shard_map/hidden_cotangent/pallas_call | solution.py:370
  124.0 2.1 copy-done.15
  126.1 1.6 copy-done.16
  127.8 1.6 fusion.35
  129.4 1.6 multiply_reduce_fusion
  131.9 1.2 collective-permute-start.12
  133.2 1.2 collective-permute-start.13
  135.6 2.0 pad_maximum_fusion.4.refs_1_
  137.6 5.9 %collective-permute-start.15 = (bf16[272,768]{1,0:T(8,128)(2,1)S(1)}, bf16[272,768]{1,0:T(8,128)(2,1)S(1)}, u32[]{:S(2)}, u32[]{:S(2)}) collective-permute-start(bf16[272,768]{1,0:T(8,128)(2,1)S(1)} %pad_maximum_fusion.6.refs_0_), channel_id=1, source_target_pairs={{0,1},{1,0},{2,3},{3,2},{4,5},{5,4},{6,7},{7,6},{8,9},{9,8},{10,11... | collective-permute-start | bytes 1253384 | tf_op jit(solution)/shard_map/ppermute | solution.py:623
  143.5 1.6 select_bitcast_fusion
  146.1 2.4 collective-permute-start.16
  148.6 5.6 %collective-permute-start.17 = (bf16[272,768]{1,0:T(8,128)(2,1)S(1)}, bf16[272,768]{1,0:T(8,128)(2,1)S(1)}, u32[]{:S(2)}, u32[]{:S(2)}) collective-permute-start(bf16[272,768]{1,0:T(8,128)(2,1)S(1)} %collective-permute-done.13.refs_2_), channel_id=1, source_target_pairs={{0,1},{1,0},{2,3},{3,2},{4,5},{5,4},{6,7},{7,6},{8,9},{9,8},{10,11... | collective-permute-start | bytes 1253384 | tf_op jit(solution)/shard_map/ppermute | solution.py:623
  154.4 2.8 multiply_sine_fusion
  159.7 25.1 %expert_pass.1 = (bf16[8,256,768]{2,1,0:T(8,128)(2,1)}, bf16[8,256,2048]{2,1,0:T(8,128)(2,1)}, bf16[8,256,1024]{2,1,0:T(8,128)(2,1)}, bf16[4,272,768]{2,1,0:T(8,...) custom-call(s32[1]{0:T(128)} %bitcast.11.e_ref, ...), custom_call_target="tpu_custom_call" | custom-call | flops 12884901888 | bytes 41943040 | tf_op jit(solution)/shard_map/expert_pass/pallas_call | solution.py:324
  189.3 3.0 fusion.8
  194.9 9.6 %bitcast_convert_fusion = bf16[768,2048]{1,0:T(8,128)(2,1)S(1)} fusion(bf16[8,256,768]{2,1,0:T(8,128)(2,1)S(1)} %copy-done.60, bf16[8,256,2048]{2,1,0:T(8,128)(2,1)} %get-tuple-element.162), kind=kOutput, calls=%fused_computation.1 | convolution fusion | flops 6444023808 | bytes 14680064 | tf_op jit(solution)/shard_map/ptd,ptf->df/dot_general | solution.py:832
  204.5 3.5 bitcast_convert_fusion.1
  208.0 2.6 pad_maximum_fusion
  210.7 1.6 collective-permute-done.24.p3
  212.3 6.4 %back_rows.1 = (f32[256,768]{1,0:T(8,128)}, bf16[256,768]{1,0:T(8,128)(2,1)}, bf16[16,64,256]{2,1,0:T(8,128)(2,1)}, f32[16,256]{1,0:T(8,128)}, f32[1,768]{1,0:T(1,128)}) custom-call(s32[2]{0:T(128)} %pad_add_fusion.2.first_ref, bf16[272,768]{1,0:T(8,128)(2,1)} %get-tuple-element.165.p0, bf16[272,768]{1,0:T(8,128)(2,1)} %copy-done.34, ...), custom_call_target="tpu_custom_call" | custom-call | flops 400000000 | bytes 5242880 | tf_op jit(solution)/shard_map/back_rows/pallas_call | solution.py:452
  218.7 2.3 convolution_convert_fusion
  221.0 3.0 collective-permute-start.26
  228.5 4.9 %all-to-all-start.2 = ((bf16[16,64,256]{2,1,0:T(8,128)(2,1)}), bf16[16,64,256]{2,1,0:T(8,128)(2,1)S(1)}, u32[]{:S(2)}, u32[]{:S(2)}) async-start(bf16[16,64,256]{2,1,0:T(8,128)(2,1)} %get-tuple-element.169), calls=%async_computation.2 | async-start | bytes 1048576 | tf_op jit(solution)/shard_map/all_to_all | solution.py:773
  233.4 2.7 pad_maximum_fusion.2
  236.2 2.8 pad_maximum_fusion.1
  238.9 2.5 fusion.12
  241.4 16.6 %all-to-all-done.2.do_ref = bf16[16,64,256]{2,1,0:T(8,128)(2,1)S(1)} async-done(((bf16[16,64,256]{2,1,0:T(8,128)(2,1)}), bf16[16,64,256]{2,1,0:T(8,128)(2,1)S(1)}, u32[]{:S(2)}, u32[]{:S(2)}) %all-to-all-start.2) | async-done | bytes 524320 | tf_op jit(solution)/shard_map/all_to_all | solution.py:773
  258.1 1.2 collective-permute-start.28
  259.5 1.5 collective-permute-start.30
  261.9 64.8 %flash_bwd.1 = (bf16[16,64,256]{2,1,0:T(8,128)(2,1)}, f32[16,128,256]{2,1,0:T(8,128)}, bf16[16,128,256]{2,1,0:T(8,128)(2,1)}) custom-call(s32[65]{0:T(128)} %copy-done.11, s32[16,1,256]{2,1,0:T(1,128)} %copy-done.8, bf16[16,192,256]{2,1,0:T(8,128)(2,1)} %copy-done.2, bf16[16,128,256]{2,1,0:T(8,128)(2,1)} %copy-done.5, bf16[16,64,256]{2,1,0:T(8,128)(2,1)} %copy-done.23, ...), custom_call_target="tpu_custom_call" | custom-call | flops 1000000000 | bytes 4194304 | tf_op jit(solution)/shard_map/flash_bwd/pallas_call | solution.py:225
  327.5 10.8 %collective-permute-start.32 = (bf16[16,128,256]{2,1,0:T(8,128)(2,1)}, bf16[16,128,256]{2,1,0:T(8,128)(2,1)S(1)}, u32[]{:S(2)}, u32[]{:S(2)}) collective-permute-start(bf16[16,128,256]{2,1,0:T(8,128)(2,1)} %get-tuple-element.190), channel_id=1, source_target_pairs={{0,1},{1,0},{2,3},{3,2},{4,5},{5,4},{6,7},{7,6},{8,9},{9,8},{10,11... | collective-permute-start | bytes 3145736 | tf_op jit(solution)/shard_map/ppermute | solution.py:623
  338.3 2.5 collective-permute-done.32.other_ref
  341.8 7.2 %head_grad.1 = bf16[16,240,256]{2,1,0:T(8,128)(2,1)} custom-call(s32[16]{0:T(128)} %broadcast_xor_fusion.at_ref, bf16[16,64,256]{2,1,0:T(8,128)(2,1)} %get-tuple-element.182.dq_ref, f32[16,128,256]{2,1,0:T(8,128)} %get-tuple-element.183.own_ref, bf16[16,128,256]{2,1,0:T(8,128)(2,1)} %copy-done.32, f32[16,32,256]{2,1,0:T(8,128)} %get-tuple-element.191.cos_ref, ...), custom_call_target="tpu_custom_call" | custom-call | flops 1200000000 | bytes 12582912 | tf_op jit(solution)/shard_map/head_grad/pallas_call | solution.py:576
  349.0 6.7 %all-to-all-start.3 = ((bf16[16,240,256]{2,1,0:T(8,128)(2,1)}), bf16[16,240,256]{2,1,0:T(8,128)(2,1)}, u32[]{:S(2)}, u32[]{:S(2)}) async-start(bf16[16,240,256]{2,1,0:T(8,128)(2,1)} %head_grad.1), calls=%async_computation.5 | async-start | bytes 3932160 | tf_op jit(solution)/shard_map/all_to_all | solution.py:773
  356.8 1.2 collective-permute-start.35
  359.6 1.9 constant_dynamic-update-slice_fusion.8
  362.4 1.8 collective-permute-start.33
  365.9 4.1 collective-permute-done.35.refs_1_
  370.0 16.7 %collective-permute-done.36.refs_2_ = bf16[48,3584]{1,0:T(8,128)(2,1)S(1)} collective-permute-done((bf16[48,3584]{1,0:T(8,128)(2,1)S(1)}, bf16[48,3584]{1,0:T(8,128)(2,1)S(1)}, u32[]{:S(2)}, u32[]{:S(2)}) %collective-permute-start.36) | collective-permute-done | bytes 344096 | tf_op jit(solution)/shard_map/ppermute | solution.py:623
  386.7 6.5 %collective-permute-done.37.refs_3_ = bf16[48,3584]{1,0:T(8,128)(2,1)S(1)} collective-permute-done((bf16[48,3584]{1,0:T(8,128)(2,1)S(1)}, bf16[48,3584]{1,0:T(8,128)(2,1)S(1)}, u32[]{:S(2)}, u32[]{:S(2)}) %collective-permute-start.37) | collective-permute-done | bytes 344096 | tf_op jit(solution)/shard_map/ppermute | solution.py:627
  393.2 1.8 finish.1
  395.7 1.8 constant_dynamic-update-slice_fusion.7
  397.5 3.1 all-to-all-done.3.arrived_ref
  401.3 1.5 slice_bitcast_fusion
  402.8 1.5 collective-permute-start.41
  407.0 5.9 %token_rows.1 = (f32[512,768]{1,0:T(8,128)}, f32[256,768]{1,0:T(8,128)}) custom-call(s32[3]{0:T(128)} %pad_add_fusion.3.first_ref, bf16[16,240,256]{2,1,0:T(8,128)(2,1)} %all-to-all-done.3.arrived_ref, bf16[3,768,384]{2,1,0:T(8,128)(2,1)} %own_ref.3, bf16[3,768,384]{2,1,0:T(8,128)(2,1)} %collective-permute-done.w_ref.other_ref, ...), custom_call_target="tpu_custom_call" | custom-call | flops 1000000000 | bytes 6291456 | tf_op jit(solution)/shard_map/token_rows/pallas_call | solution.py:489
  412.9 1.5 copy.90
  414.4 1.3 dynamic-slice_divide_fusion
  (292 shorter events, 51.9 us)
Async XLA Ops:
  7.2 100.3 %all-gather.3.cloned.1.call-start = ((), (), s32[]{:S(2)}) async-start(), calls=%async_computation.8 | async-start | bytes 3538944 | tf_op jit(solution)/shard_map/all_gather | solution.py:780
  7.2 5.1 %collective-permute-start = (bf16[3,768,384]{2,1,0:T(8,128)(2,1)}, bf16[3,768,384]{2,1,0:T(8,128)(2,1)}, u32[]{:S(2)}, u32[]{:S(2)}) collective-permute-start(bf16[3,768,384]{2,1,0:T(8,128)(2,1)} %own_ref.3), channel_id=1, source_target_pairs={{0,1},{1,0},{2,3},{3,2},{4,5},{5,4},{6,7},{7,6},{8,9},{9,8},{10,11... | collective-permute-start | bytes 5308424 | tf_op jit(solution)/shard_map/ppermute | solution.py:623
  8.8 120.7 %copy-start.3 = (bf16[256,768]{1,0:T(8,128)(2,1)}, bf16[256,768]{1,0:T(8,128)(2,1)S(1)}, u32[]{:S(2)}) copy-start(bf16[256,768]{1,0:T(8,128)(2,1)S(1)} %constant_dynamic-slice_fusion.6.x_ref) | copy-start | bytes 1179652
  16.1 45.7 %all-to-all-start = ((bf16[16,192,256]{2,1,0:T(8,128)(2,1)}), bf16[16,192,256]{2,1,0:T(8,128)(2,1)S(1)}, u32[]{:S(2)}, u32[]{:S(2)}) async-start(bf16[16,192,256]{2,1,0:T(8,128)(2,1)} %get-tuple-element.120), calls=%async_computation | async-start | bytes 3145728 | tf_op jit(solution)/shard_map/all_to_all | solution.py:773
  23.3 44.8 %copy-start.56 = (s32[512,2]{0,1:T(2,128)S(1)}, s32[512,2]{0,1:T(2,128)}, u32[]{:S(2)}) copy-start(s32[512,2]{0,1:T(2,128)} %param.18) | copy-start | bytes 12292
  23.3 44.8 %copy-start.58 = (s32[8]{0:T(128)S(1)}, s32[8]{0:T(128)}, u32[]{:S(2)}) copy-start(s32[8]{0:T(128)} %constant.158.clone) | copy-start | bytes 100
  23.3 106.1 %collective-permute-start.11 = (bf16[384,768]{1,0:T(8,128)(2,1)}, bf16[384,768]{1,0:T(8,128)(2,1)}, u32[]{:S(2)}, u32[]{:S(2)}) collective-permute-start(bf16[384,768]{1,0:T(8,128)(2,1)} %own_ref.2), channel_id=1, source_target_pairs={{0,1},{1,0},{2,3},{3,2},{4,5},{5,4},{6,7},{7,6},{8,9},{9,8},{10,11... | collective-permute-start | bytes 1769480 | tf_op jit(solution)/shard_map/ppermute | solution.py:623
  24.3 6.9 %collective-permute-start.2 = (s32[512]{0:T(512)S(1)}, s32[512]{0:T(512)S(1)}, u32[]{:S(2)}, u32[]{:S(2)}) collective-permute-start(s32[512]{0:T(512)S(1)} %copy-done.55), channel_id=1, source_target_pairs={{0,4},{4,0},{1,5},{5,1},{2,6},{6,2},{3,7},{7,3},{8,12},{12,8},{9,1... | collective-permute-start | bytes 6152 | tf_op jit(solution)/shard_map/ppermute | solution.py:623
  25.5 6.4 %collective-permute-start.3 = (s32[512]{0:T(512)S(1)}, s32[512]{0:T(512)S(1)}, u32[]{:S(2)}, u32[]{:S(2)}) collective-permute-start(s32[512]{0:T(512)S(1)} %copy-done.55), channel_id=1, source_target_pairs={{0,6},{2,4},{4,2},{6,0},{1,7},{3,5},{5,3},{7,1},{8,14},{10,12},{12... | collective-permute-start | bytes 6152 | tf_op jit(solution)/shard_map/ppermute | solution.py:627
  26.7 5.3 %collective-permute-start.1 = (s32[512]{0:T(512)S(1)}, s32[512]{0:T(512)S(1)}, u32[]{:S(2)}, u32[]{:S(2)}) collective-permute-start(s32[512]{0:T(512)S(1)} %copy-done.55), channel_id=1, source_target_pairs={{0,2},{2,0},{1,3},{3,1},{4,6},{6,4},{5,7},{7,5},{8,10},{10,8},{9,1... | collective-permute-start | bytes 6152 | tf_op jit(solution)/shard_map/ppermute | solution.py:623
  32.0 18.4 %collective-permute-start.4 = (s32[2048]{0:T(1024)S(1)}, s32[2048]{0:T(1024)S(1)}, u32[]{:S(2)}, u32[]{:S(2)}) collective-permute-start(s32[2048]{0:T(1024)S(1)} %bitcast.126), channel_id=1, source_target_pairs={{0,8},{8,0},{16,24},{24,16},{1,9},{9,1},{17,25},{25,17},{2,10},{10... | collective-permute-start | bytes 24584 | tf_op jit(solution)/shard_map/ppermute | solution.py:642
  37.2 20.1 %collective-permute-start.5 = (s32[2048]{0:T(1024)S(1)}, s32[2048]{0:T(1024)S(1)}, u32[]{:S(2)}, u32[]{:S(2)}) collective-permute-start(s32[2048]{0:T(1024)S(1)} %bitcast.127), channel_id=1, source_target_pairs={{0,16},{8,24},{16,0},{24,8},{1,17},{9,25},{17,1},{25,9},{2,18},{10... | collective-permute-start | bytes 24584 | tf_op jit(solution)/shard_map/ppermute | solution.py:642
  37.2 21.5 %collective-permute-start.6 = (s32[2048]{0:T(1024)S(1)}, s32[2048]{0:T(1024)S(1)}, u32[]{:S(2)}, u32[]{:S(2)}) collective-permute-start(s32[2048]{0:T(1024)S(1)} %bitcast.128), channel_id=1, source_target_pairs={{0,24},{8,16},{16,8},{24,0},{1,25},{9,17},{17,9},{25,1},{2,26},{10... | collective-permute-start | bytes 24584 | tf_op jit(solution)/shard_map/ppermute | solution.py:642
  61.7 42.7 %copy-start.2 = (bf16[16,192,256]{2,1,0:T(8,128)(2,1)}, bf16[16,192,256]{2,1,0:T(8,128)(2,1)S(1)}, u32[]{:S(2)}) copy-start(bf16[16,192,256]{2,1,0:T(8,128)(2,1)S(1)} %all-to-all-done.own_ref) | copy-start | bytes 4718596
  62.9 5.3 %collective-permute-start.7 = (bf16[16,128,256]{2,1,0:T(8,128)(2,1)}, bf16[16,128,256]{2,1,0:T(8,128)(2,1)S(1)}, u32[]{:S(2)}, u32[]{:S(2)}) collective-permute-start(bf16[16,128,256]{2,1,0:T(8,128)(2,1)} %slice.179), channel_id=1, source_target_pairs={{0,1},{1,0},{2,3},{3,2},{4,5},{5,4},{6,7},{7,6},{8,9},{9,8},{10,11... | collective-permute-start | bytes 3145736 | tf_op jit(solution)/shard_map/ppermute | solution.py:623
  64.3 40.1 %copy-start.8 = (s32[16,1,256]{2,1,0:T(1,128)}, s32[16,1,256]{2,1,0:T(1,128)S(1)}, u32[]{:S(2)}) copy-start(s32[16,1,256]{2,1,0:T(1,128)S(1)} %dynamic-slice_maximum_fusion.start_ref) | copy-start | bytes 49156
  64.9 39.5 %copy-start.11 = (s32[65]{0:T(128)}, s32[65]{0:T(128)S(1)}, u32[]{:S(2)}) copy-start(s32[65]{0:T(128)S(1)} %concatenate.103.sc) | copy-start | bytes 784
  64.9 41.1 %collective-permute-start.10 = (bf16[256,768]{1,0:T(8,128)(2,1)S(1)}, bf16[256,768]{1,0:T(8,128)(2,1)S(1)}, u32[]{:S(2)}, u32[]{:S(2)}) collective-permute-start(bf16[256,768]{1,0:T(8,128)(2,1)S(1)} %get-tuple-element.133), channel_id=1, source_target_pairs={{0,24},{8,16},{16,8},{24,0},{1,25},{9,17},{17,9},{25,1},{2,26},{10... | collective-permute-start | bytes 1179656 | tf_op jit(solution)/shard_map/ppermute | solution.py:642
  66.0 40.1 %collective-permute-start.8 = (bf16[256,768]{1,0:T(8,128)(2,1)S(1)}, bf16[256,768]{1,0:T(8,128)(2,1)S(1)}, u32[]{:S(2)}, u32[]{:S(2)}) collective-permute-start(bf16[256,768]{1,0:T(8,128)(2,1)S(1)} %get-tuple-element.133), channel_id=1, source_target_pairs={{0,8},{8,0},{16,24},{24,16},{1,9},{9,1},{17,25},{25,17},{2,10},{10... | collective-permute-start | bytes 1179656 | tf_op jit(solution)/shard_map/ppermute | solution.py:642
  68.0 39.6 %collective-permute-start.9 = (bf16[256,768]{1,0:T(8,128)(2,1)S(1)}, bf16[256,768]{1,0:T(8,128)(2,1)}, u32[]{:S(2)}, u32[]{:S(2)}) collective-permute-start(bf16[256,768]{1,0:T(8,128)(2,1)S(1)} %get-tuple-element.133), channel_id=1, source_target_pairs={{0,16},{8,24},{16,0},{24,8},{1,17},{9,25},{17,1},{25,9},{2,18},{10... | collective-permute-start | bytes 1179656 | tf_op jit(solution)/shard_map/ppermute | solution.py:642
  68.1 46.5 %copy-start.52 = (bf16[768,8]{0,1:T(8,128)(2,1)S(1)}, bf16[768,8]{0,1:T(8,128)(2,1)}, u32[]{:S(2)}) copy-start(bf16[768,8]{0,1:T(8,128)(2,1)} %param.24) | copy-start | bytes 36868
  68.1 46.5 %copy-start.53 = (bf16[768,4]{0,1:T(4,128)(2,1)S(1)}, bf16[768,4]{0,1:T(4,128)(2,1)}, u32[]{:S(2)}) copy-start(bf16[768,4]{0,1:T(4,128)(2,1)} %param.25) | copy-start | bytes 18436
  68.1 46.6 %copy-start.57 = (s32[16]{0:T(128)S(1)}, s32[16]{0:T(128)}, u32[]{:S(2)}) copy-start(s32[16]{0:T(128)} %constant.159.clone) | copy-start | bytes 196
  68.2 36.3 %copy-start.5 = (bf16[16,128,256]{2,1,0:T(8,128)(2,1)}, bf16[16,128,256]{2,1,0:T(8,128)(2,1)S(1)}, u32[]{:S(2)}) copy-start(bf16[16,128,256]{2,1,0:T(8,128)(2,1)S(1)} %collective-permute-done.7.oth_ref) | copy-start | bytes 3145732
  107.5 20.2 %all-to-all-start.1 = ((bf16[16,64,256]{2,1,0:T(8,128)(2,1)}), bf16[16,64,256]{2,1,0:T(8,128)(2,1)S(1)}, u32[]{:S(2)}, u32[]{:S(2)}) async-start(bf16[16,64,256]{2,1,0:T(8,128)(2,1)} %get-tuple-element.128), calls=%async_computation.1 | async-start | bytes 1048576 | tf_op jit(solution)/shard_map/all_to_all | solution.py:773
  114.3 234.6 %reduce-scatter.5.cloned.1.call-start = ((), (), s32[]{:S(2)}) async-start(), calls=%async_computation.7 | async-start | bytes 983040 | tf_op jit(solution)/shard_map/reduce_scatter | solution.py:877
  131.9 14.2 %collective-permute-start.12 = (bf16[272,768]{1,0:T(8,128)(2,1)S(1)}, bf16[272,768]{1,0:T(8,128)(2,1)S(1)}, u32[]{:S(2)}, u32[]{:S(2)}) collective-permute-start(bf16[272,768]{1,0:T(8,128)(2,1)S(1)} %pad_maximum_fusion.6.refs_0_), channel_id=1, source_target_pairs={{0,2},{2,0},{1,3},{3,1},{4,6},{6,4},{5,7},{7,5},{8,10},{10,8},{9,1... | collective-permute-start | bytes 1253384 | tf_op jit(solution)/shard_map/ppermute | solution.py:623
  133.2 15.4 %collective-permute-start.13 = (bf16[272,768]{1,0:T(8,128)(2,1)S(1)}, bf16[272,768]{1,0:T(8,128)(2,1)S(1)}, u32[]{:S(2)}, u32[]{:S(2)}) collective-permute-start(bf16[272,768]{1,0:T(8,128)(2,1)S(1)} %pad_maximum_fusion.6.refs_0_), channel_id=1, source_target_pairs={{0,4},{4,0},{1,5},{5,1},{2,6},{6,2},{3,7},{7,3},{8,12},{12,8},{9,1... | collective-permute-start | bytes 1253384 | tf_op jit(solution)/shard_map/ppermute | solution.py:623
  134.4 19.8 %collective-permute-start.14 = (bf16[272,768]{1,0:T(8,128)(2,1)S(1)}, bf16[272,768]{1,0:T(8,128)(2,1)S(1)}, u32[]{:S(2)}, u32[]{:S(2)}) collective-permute-start(bf16[272,768]{1,0:T(8,128)(2,1)S(1)} %pad_maximum_fusion.6.refs_0_), channel_id=1, source_target_pairs={{0,6},{2,4},{4,2},{6,0},{1,7},{3,5},{5,3},{7,1},{8,14},{10,12},{12... | collective-permute-start | bytes 1253384 | tf_op jit(solution)/shard_map/ppermute | solution.py:627
  137.6 19.6 %collective-permute-start.15 = (bf16[272,768]{1,0:T(8,128)(2,1)S(1)}, bf16[272,768]{1,0:T(8,128)(2,1)S(1)}, u32[]{:S(2)}, u32[]{:S(2)}) collective-permute-start(bf16[272,768]{1,0:T(8,128)(2,1)S(1)} %pad_maximum_fusion.6.refs_0_), channel_id=1, source_target_pairs={{0,1},{1,0},{2,3},{3,2},{4,5},{5,4},{6,7},{7,6},{8,9},{9,8},{10,11... | collective-permute-start | bytes 1253384 | tf_op jit(solution)/shard_map/ppermute | solution.py:623
  146.1 11.0 %collective-permute-start.16 = (bf16[272,768]{1,0:T(8,128)(2,1)S(1)}, bf16[272,768]{1,0:T(8,128)(2,1)S(1)}, u32[]{:S(2)}, u32[]{:S(2)}) collective-permute-start(bf16[272,768]{1,0:T(8,128)(2,1)S(1)} %collective-permute-done.12.refs_1_), channel_id=1, source_target_pairs={{0,1},{1,0},{2,3},{3,2},{4,5},{5,4},{6,7},{7,6},{8,9},{9,8},{10,11... | collective-permute-start | bytes 1253384 | tf_op jit(solution)/shard_map/ppermute | solution.py:623
  148.6 8.5 %collective-permute-start.17 = (bf16[272,768]{1,0:T(8,128)(2,1)S(1)}, bf16[272,768]{1,0:T(8,128)(2,1)S(1)}, u32[]{:S(2)}, u32[]{:S(2)}) collective-permute-start(bf16[272,768]{1,0:T(8,128)(2,1)S(1)} %collective-permute-done.13.refs_2_), channel_id=1, source_target_pairs={{0,1},{1,0},{2,3},{3,2},{4,5},{5,4},{6,7},{7,6},{8,9},{9,8},{10,11... | collective-permute-start | bytes 1253384 | tf_op jit(solution)/shard_map/ppermute | solution.py:623
  154.2 2.9 collective-permute-start.18
  157.2 27.7 %collective-permute-start.19 = (bf16[2,256,768]{2,1,0:T(8,128)(2,1)}, bf16[2,256,768]{2,1,0:T(8,128)(2,1)}, u32[]{:S(2)}, u32[]{:S(2)}) collective-permute-start(bf16[2,256,768]{2,1,0:T(8,128)(2,1)} %pad_maximum_fusion.3.refs_0_), channel_id=1, source_target_pairs={{0,2},{2,0},{1,3},{3,1},{4,6},{6,4},{5,7},{7,5},{8,10},{10,8},{9,1... | collective-permute-start | bytes 2359304 | tf_op jit(solution)/shard_map/ppermute | solution.py:623
  158.0 26.8 %collective-permute-start.20 = (bf16[2,256,768]{2,1,0:T(8,128)(2,1)}, bf16[2,256,768]{2,1,0:T(8,128)(2,1)}, u32[]{:S(2)}, u32[]{:S(2)}) collective-permute-start(bf16[2,256,768]{2,1,0:T(8,128)(2,1)} %pad_maximum_fusion.4.refs_1_), channel_id=1, source_target_pairs={{0,4},{4,0},{1,5},{5,1},{2,6},{6,2},{3,7},{7,3},{8,12},{12,8},{9,1... | collective-permute-start | bytes 2359304 | tf_op jit(solution)/shard_map/ppermute | solution.py:623
  159.7 26.8 %copy-start.50 = (f32[2,768]{1,0:T(2,128)S(1)}, f32[2,768]{1,0:T(2,128)}, u32[]{:S(2)}) copy-start(f32[2,768]{1,0:T(2,128)} %param.26) | copy-start | bytes 18436
  184.8 4.4 %collective-permute-start.21 = (bf16[4,272,768]{2,1,0:T(8,128)(2,1)}, bf16[4,272,768]{2,1,0:T(8,128)(2,1)S(1)}, u32[]{:S(2)}, u32[]{:S(2)}) collective-permute-start(bf16[4,272,768]{2,1,0:T(8,128)(2,1)} %get-tuple-element.154), channel_id=1, source_target_pairs={{0,1},{1,0},{2,3},{3,2},{4,5},{5,4},{6,7},{7,6},{8,9},{9,8},{10,11... | collective-permute-start | bytes 5013512 | tf_op jit(solution)/shard_map/ppermute | solution.py:623
  192.2 18.4 %collective-permute-start.22 = (bf16[272,768]{1,0:T(8,128)(2,1)}, bf16[272,768]{1,0:T(8,128)(2,1)S(1)}, u32[]{:S(2)}, u32[]{:S(2)}) collective-permute-start(bf16[272,768]{1,0:T(8,128)(2,1)} %get-tuple-element.158), channel_id=1, source_target_pairs={{0,2},{2,0},{1,3},{3,1},{4,6},{6,4},{5,7},{7,5},{8,10},{10,8},{9,1... | collective-permute-start | bytes 1253384 | tf_op jit(solution)/shard_map/ppermute | solution.py:623
  193.4 17.3 %collective-permute-start.23 = (bf16[272,768]{1,0:T(8,128)(2,1)}, bf16[272,768]{1,0:T(8,128)(2,1)S(1)}, u32[]{:S(2)}, u32[]{:S(2)}) collective-permute-start(bf16[272,768]{1,0:T(8,128)(2,1)} %get-tuple-element.159), channel_id=1, source_target_pairs={{0,4},{4,0},{1,5},{5,1},{2,6},{6,2},{3,7},{7,3},{8,12},{12,8},{9,1... | collective-permute-start | bytes 1253384 | tf_op jit(solution)/shard_map/ppermute | solution.py:623
  193.7 18.6 %collective-permute-start.24 = (bf16[272,768]{1,0:T(8,128)(2,1)}, bf16[272,768]{1,0:T(8,128)(2,1)}, u32[]{:S(2)}, u32[]{:S(2)}) collective-permute-start(bf16[272,768]{1,0:T(8,128)(2,1)} %get-tuple-element.160), channel_id=1, source_target_pairs={{0,6},{2,4},{4,2},{6,0},{1,7},{3,5},{5,3},{7,1},{8,14},{10,12},{12... | collective-permute-start | bytes 1253384 | tf_op jit(solution)/shard_map/ppermute | solution.py:627
  210.6 14.3 %copy-start.22 = (bf16[256,768]{1,0:T(8,128)(2,1)S(1)}, bf16[256,768]{1,0:T(8,128)(2,1)}, u32[]{:S(2)}) copy-start(bf16[256,768]{1,0:T(8,128)(2,1)} %copy-done.21) | copy-start | bytes 1179652
  221.0 5.3 %collective-permute-start.26 = (bf16[768,384]{1,0:T(8,128)(2,1)}, bf16[768,384]{1,0:T(8,128)(2,1)S(1)}, u32[]{:S(2)}, u32[]{:S(2)}) collective-permute-start(bf16[768,384]{1,0:T(8,128)(2,1)} %convolution_convert_fusion), channel_id=1, source_target_pairs={{0,1},{1,0},{2,3},{3,2},{4,5},{5,4},{6,7},{7,6},{8,9},{9,8},{10,11... | collective-permute-start | bytes 1769480 | tf_op jit(solution)/shard_map/ppermute | solution.py:623
  227.7 121.3 %reduce-scatter.3.cloned.1.call-start = ((), (), s32[]{:S(2)}) async-start(), calls=%async_computation.6 | async-start | bytes 5898240 | tf_op jit(solution)/shard_map/reduce_scatter | solution.py:836
  228.4 10.5 %collective-permute-start.25 = (bf16[4,256,768]{2,1,0:T(8,128)(2,1)}, bf16[4,256,768]{2,1,0:T(8,128)(2,1)}, u32[]{:S(2)}, u32[]{:S(2)}) collective-permute-start(bf16[4,256,768]{2,1,0:T(8,128)(2,1)} %get-tuple-element.172), channel_id=1, source_target_pairs={{0,1},{1,0},{2,3},{3,2},{4,5},{5,4},{6,7},{7,6},{8,9},{9,8},{10,11... | collective-permute-start | bytes 4718600 | tf_op jit(solution)/shard_map/ppermute | solution.py:623
  228.5 29.6 %all-to-all-start.2 = ((bf16[16,64,256]{2,1,0:T(8,128)(2,1)}), bf16[16,64,256]{2,1,0:T(8,128)(2,1)S(1)}, u32[]{:S(2)}, u32[]{:S(2)}) async-start(bf16[16,64,256]{2,1,0:T(8,128)(2,1)} %get-tuple-element.169), calls=%async_computation.2 | async-start | bytes 1048576 | tf_op jit(solution)/shard_map/all_to_all | solution.py:773
  258.1 68.7 %collective-permute-start.27 = (bf16[2,2,256,768]{3,2,1,0:T(8,128)(2,1)}, bf16[2,2,256,768]{3,2,1,0:T(8,128)(2,1)S(1)}, u32[]{:S(2)}, u32[]{:S(2)}) collective-permute-start(bf16[2,2,256,768]{3,2,1,0:T(8,128)(2,1)} %pad_maximum_fusion.1), channel_id=1, source_target_pairs={{0,4},{4,0},{1,5},{5,1},{2,6},{6,2},{3,7},{7,3},{8,12},{12,8},{9,1... | collective-permute-start | bytes 4718600 | tf_op jit(solution)/shard_map/ppermute | solution.py:623
  258.1 68.7 %collective-permute-start.28 = (bf16[2,2,256,768]{3,2,1,0:T(8,128)(2,1)}, bf16[2,2,256,768]{3,2,1,0:T(8,128)(2,1)}, u32[]{:S(2)}, u32[]{:S(2)}) collective-permute-start(bf16[2,2,256,768]{3,2,1,0:T(8,128)(2,1)} %pad_maximum_fusion.2), channel_id=1, source_target_pairs={{0,2},{2,0},{1,3},{3,1},{4,6},{6,4},{5,7},{7,5},{8,10},{10,8},{9,1... | collective-permute-start | bytes 4718600 | tf_op jit(solution)/shard_map/ppermute | solution.py:623
  259.3 67.4 %collective-permute-start.29 = (bf16[256,768]{1,0:T(8,128)(2,1)S(1)}, bf16[256,768]{1,0:T(8,128)(2,1)S(1)}, u32[]{:S(2)}, u32[]{:S(2)}) collective-permute-start(bf16[256,768]{1,0:T(8,128)(2,1)S(1)} %get-tuple-element.187), channel_id=1, source_target_pairs={{0,2},{2,0},{1,3},{3,1},{4,6},{6,4},{5,7},{7,5},{8,10},{10,8},{9,1... | collective-permute-start | bytes 1179656 | tf_op jit(solution)/shard_map/ppermute | solution.py:623
  259.5 67.2 %collective-permute-start.30 = (bf16[256,768]{1,0:T(8,128)(2,1)S(1)}, bf16[256,768]{1,0:T(8,128)(2,1)S(1)}, u32[]{:S(2)}, u32[]{:S(2)}) collective-permute-start(bf16[256,768]{1,0:T(8,128)(2,1)S(1)} %get-tuple-element.188), channel_id=1, source_target_pairs={{0,4},{4,0},{1,5},{5,1},{2,6},{6,2},{3,7},{7,3},{8,12},{12,8},{9,1... | collective-permute-start | bytes 1179656 | tf_op jit(solution)/shard_map/ppermute | solution.py:623
  261.0 65.7 %collective-permute-start.31 = (bf16[256,768]{1,0:T(8,128)(2,1)S(1)}, bf16[256,768]{1,0:T(8,128)(2,1)S(1)}, u32[]{:S(2)}, u32[]{:S(2)}) collective-permute-start(bf16[256,768]{1,0:T(8,128)(2,1)S(1)} %get-tuple-element.189), channel_id=1, source_target_pairs={{0,6},{2,4},{4,2},{6,0},{1,7},{3,5},{5,3},{7,1},{8,14},{10,12},{12... | collective-permute-start | bytes 1179656 | tf_op jit(solution)/shard_map/ppermute | solution.py:627
  261.9 76.4 %copy-start.49 = (f32[16,256]{1,0:T(8,128)S(1)}, f32[16,256]{1,0:T(8,128)}, u32[]{:S(2)}) copy-start(f32[16,256]{1,0:T(8,128)} %get-tuple-element.175) | copy-start | bytes 49156
  326.7 14.1 %copy-start.42 = (bf16[256,768]{1,0:T(8,128)(2,1)}, bf16[256,768]{1,0:T(8,128)(2,1)S(1)}, u32[]{:S(2)}) copy-start(bf16[256,768]{1,0:T(8,128)(2,1)S(1)} %collective-permute-done.30) | copy-start | bytes 1179652
  327.5 13.3 %collective-permute-start.32 = (bf16[16,128,256]{2,1,0:T(8,128)(2,1)}, bf16[16,128,256]{2,1,0:T(8,128)(2,1)S(1)}, u32[]{:S(2)}, u32[]{:S(2)}) collective-permute-start(bf16[16,128,256]{2,1,0:T(8,128)(2,1)} %get-tuple-element.190), channel_id=1, source_target_pairs={{0,1},{1,0},{2,3},{3,2},{4,5},{5,4},{6,7},{7,6},{8,9},{9,8},{10,11... | collective-permute-start | bytes 3145736 | tf_op jit(solution)/shard_map/ppermute | solution.py:623
  349.0 51.6 %all-to-all-start.3 = ((bf16[16,240,256]{2,1,0:T(8,128)(2,1)}), bf16[16,240,256]{2,1,0:T(8,128)(2,1)}, u32[]{:S(2)}, u32[]{:S(2)}) async-start(bf16[16,240,256]{2,1,0:T(8,128)(2,1)} %head_grad.1), calls=%async_computation.5 | async-start | bytes 3932160 | tf_op jit(solution)/shard_map/all_to_all | solution.py:773
  356.8 13.2 %collective-permute-start.35 = (bf16[48,3584]{1,0:T(8,128)(2,1)S(1)}, bf16[48,3584]{1,0:T(8,128)(2,1)S(1)}, u32[]{:S(2)}, u32[]{:S(2)}) collective-permute-start(bf16[48,3584]{1,0:T(8,128)(2,1)S(1)} %get-tuple-element.306), channel_id=1, source_target_pairs={{0,2},{2,0},{1,3},{3,1},{4,6},{6,4},{5,7},{7,5},{8,10},{10,8},{9,1... | collective-permute-start | bytes 1032200 | tf_op jit(solution)/shard_map/ppermute | solution.py:623
  358.0 28.6 %collective-permute-start.36 = (bf16[48,3584]{1,0:T(8,128)(2,1)S(1)}, bf16[48,3584]{1,0:T(8,128)(2,1)S(1)}, u32[]{:S(2)}, u32[]{:S(2)}) collective-permute-start(bf16[48,3584]{1,0:T(8,128)(2,1)S(1)} %get-tuple-element.305), channel_id=1, source_target_pairs={{0,4},{4,0},{1,5},{5,1},{2,6},{6,2},{3,7},{7,3},{8,12},{12,8},{9,1... | collective-permute-start | bytes 1032200 | tf_op jit(solution)/shard_map/ppermute | solution.py:623
  359.2 34.0 %collective-permute-start.37 = (bf16[48,3584]{1,0:T(8,128)(2,1)S(1)}, bf16[48,3584]{1,0:T(8,128)(2,1)S(1)}, u32[]{:S(2)}, u32[]{:S(2)}) collective-permute-start(bf16[48,3584]{1,0:T(8,128)(2,1)S(1)} %get-tuple-element.304), channel_id=1, source_target_pairs={{0,6},{2,4},{4,2},{6,0},{1,7},{3,5},{5,3},{7,1},{8,14},{10,12},{12... | collective-permute-start | bytes 1032200 | tf_op jit(solution)/shard_map/ppermute | solution.py:627
  362.4 33.3 %collective-permute-start.33 = (bf16[256,768]{1,0:T(8,128)(2,1)}, bf16[256,768]{1,0:T(8,128)(2,1)}, u32[]{:S(2)}, u32[]{:S(2)}) collective-permute-start(bf16[256,768]{1,0:T(8,128)(2,1)} %get-tuple-element.325), channel_id=1, source_target_pairs={{0,1},{1,0},{2,3},{3,2},{4,5},{5,4},{6,7},{7,6},{8,9},{9,8},{10,11... | collective-permute-start | bytes 1179656 | tf_op jit(solution)/shard_map/ppermute | solution.py:623
  364.7 1.2 collective-permute-start.34
  365.9 47.0 %copy-start.51 = (f32[512,8]{0,1:T(8,128)}, f32[512,8]{0,1:T(8,128)S(1)}, u32[]{:S(2)}) copy-start(f32[512,8]{0,1:T(8,128)S(1)} %constant_dynamic-update-slice_fusion.5) | copy-start | bytes 49156
  402.8 12.8 %collective-permute-start.41 = (f32[48,128]{1,0:T(8,128)S(1)}, f32[48,128]{1,0:T(8,128)S(1)}, u32[]{:S(2)}, u32[]{:S(2)}) collective-permute-start(f32[48,128]{1,0:T(8,128)S(1)} %slice.170), channel_id=1, source_target_pairs={{0,1},{1,0},{2,3},{3,2},{4,5},{5,4},{6,7},{7,6},{8,9},{9,8},{10,11... | collective-permute-start | bytes 73736 | tf_op jit(solution)/shard_map/ppermute | solution.py:623
  406.4 12.8 %collective-permute-start.40 = (bf16[6,48,192]{2,1,0:T(8,128)(2,1)S(1)}, bf16[6,48,192]{2,1,0:T(8,128)(2,1)S(1)}, u32[]{:S(2)}, u32[]{:S(2)}) collective-permute-start(bf16[6,48,192]{2,1,0:T(8,128)(2,1)S(1)} %constant_dynamic-slice_fusion), channel_id=1, source_target_pairs={{0,1},{1,0},{2,3},{3,2},{4,5},{5,4},{6,7},{7,6},{8,9},{9,8},{10,11... | collective-permute-start | bytes 331784 | tf_op jit(solution)/shard_map/ppermute | solution.py:623
  406.5 7.9 %collective-permute-start.39 = (f32[48]{0:T(128)S(1)}, f32[48]{0:T(128)S(1)}, u32[]{:S(2)}, u32[]{:S(2)}) collective-permute-start(f32[48]{0:T(128)S(1)} %convert_reduce_fusion), channel_id=1, source_target_pairs={{0,1},{1,0},{2,3},{3,2},{4,5},{5,4},{6,7},{7,6},{8,9},{9,8},{10,11... | collective-permute-start | bytes 584 | tf_op jit(solution)/shard_map/ppermute | solution.py:623
  412.9 8.7 %collective-permute-start.38 = (f32[256,768]{1,0:T(8,128)}, f32[256,768]{1,0:T(8,128)S(1)}, u32[]{:S(2)}, u32[]{:S(2)}) collective-permute-start(f32[256,768]{1,0:T(8,128)} %get-tuple-element.217), channel_id=1, source_target_pairs={{0,1},{1,0},{2,3},{3,2},{4,5},{5,4},{6,7},{7,6},{8,9},{9,8},{10,11... | collective-permute-start | bytes 2359304 | tf_op jit(solution)/shard_map/ppermute | solution.py:623
  (46 other events, 182.1 us)
Sparse Core Ops, SparseCore 0:
  16.2 50.5 all-gather.2
  227.8 30.1 reduce-scatter.4
  260.4 85.9 reduce-scatter.2
